TPU v7x, 32 devices: a whole 2x2x4 slice. The times are simulated.
32 devices in a mesh: scene: 4 (over y, x), row: 4 (over z), col: 2 (over core).
Axes of the slice: x: 2, y: 2, z: 4, core: 2. Of those that a mesh axis runs over, the one named last changes fastest.
Arguments:
- scenes: bfloat16 [4, 256, 128, 128], P('scene', 'row', 'col'), may hold values from -6 to 6
- cotangent: bfloat16 [4, 256, 128, 128], P('scene', 'row', 'col'), may hold values from -0.016479492 to 0.016479492
- params: float32 [294912], P(('scene', 'row', 'col')), may hold values from -0.1875 to 0.1875
- partials: float32 [32, 294912], P(('scene', 'row', 'col')), may hold values from -8 to 8
Outputs:
- sam_grad: float32 [294912], P(('scene', 'row', 'col'))
All inputs are finite; a program needn't handle non-finite values.
Results may differ from a plain program's by a relative error of at most 0.0042.
Values may be sent and summed in bfloat16 or wider, within the bound.
A program may use at most 64 MiB of HBM per device.

v0:
```python
import jax
import jax.numpy as jnp
from jax import lax
from jax.sharding import PartitionSpec as P

radius = 2.0
epsilon = 1e-06


def with_halo(cells, sides, width):
    for axis, dim in sides:
        count = lax.axis_size(axis)
        ends = count - 1
        head = lax.slice_in_dim(cells, 0, width, axis=dim)
        tail = lax.slice_in_dim(cells, cells.shape[dim] - width, cells.shape[dim], axis=dim)
        cells = jnp.concatenate(
            [
                lax.ppermute(tail, axis, [(i, (i + 1) % count) for i in range(ends)]),
                cells,
                lax.ppermute(head, axis, [((i + 1) % count, i) for i in range(ends)]),
            ],
            axis=dim,
        )
    return cells


def convolve(padded, kernel):
    return lax.conv_general_dilated(
        padded,
        kernel,
        (1, 1),
        "VALID",
        dimension_numbers=("NHWC", "HWIO", "NHWC"),
        preferred_element_type=jnp.float32,
    )


def widened(field):
    return with_halo(field, (("row", 1), ("col", 2)), 1)


def kernel_grad(padded, errors):
    height = errors.shape[1]
    width = errors.shape[2]
    rows_out = []
    for row_off in range(3):
        cols_out = []
        for col_off in range(3):
            window = padded[:, row_off : row_off + height, col_off : col_off + width, :]
            cols_out.append(
                jnp.einsum("nhwc,nhwd->cd", window, errors, preferred_element_type=jnp.float32)
            )
        rows_out.append(jnp.stack(cols_out))
    return jnp.stack(rows_out)


def on_device(scenes, cotangent, params, partials):
    local_part = partials[0]
    totals = lax.psum(local_part, ("scene", "row", "col"))
    raw_whole = lax.all_gather(params, ("scene", "row", "col"), axis=0, tiled=True)
    factor = radius / (jnp.sqrt(jnp.sum(totals * totals)) + epsilon)
    whole = (raw_whole + factor * totals).astype(jnp.bfloat16)
    channels = scenes.shape[3]
    kernels = whole.reshape(2, 3, 3, channels, channels)
    kernel_one = kernels[0]
    flipped = jnp.transpose(kernels[1][::-1, ::-1], (0, 1, 3, 2))
    padded_in = widened(scenes)
    pre = convolve(padded_in, kernel_one)
    hidden = jax.nn.silu(pre).astype(jnp.bfloat16)
    back = convolve(widened(cotangent), flipped)
    squash = jax.nn.sigmoid(pre)
    delta = (back * squash * (1.0 + pre * (1.0 - squash))).astype(jnp.bfloat16)
    grad_one = kernel_grad(padded_in, delta)
    grad_two = kernel_grad(widened(hidden), cotangent)
    local_grad = jnp.stack([grad_one, grad_two]).reshape(-1)
    return lax.psum_scatter(local_grad, ("scene", "row", "col"), scatter_dimension=0, tiled=True)


def solution(mesh):
    return jax.shard_map(
        on_device,
        mesh=mesh,
        in_specs=(
            P("scene", "row", "col", None),
            P("scene", "row", "col", None),
            P(("scene", "row", "col")),
            P(("scene", "row", "col"), None),
        ),
        out_specs=P(("scene", "row", "col")),
        check_vma=False,
    )
```

profile of v0, /device:TPU:0, one launch (start us, length us, event | category | flops | bytes accessed | tf_op | source)
XLA Modules:
  0.0 384.6 jit_solution(3427847306633833855)
XLA Ops:
  8.1 5.1 %collective-permute-start = (bf16[1,1,64,128]{3,2,1,0:T(8,128)(2,1)S(1)}, bf16[1,1,64,128]{3,2,1,0:T(8,128)(2,1)S(1)}, u32[]{:S(2)}, u32[]{:S(2)}) collective-permute-start(bf16[1,1,64,128]{3,2,1,0:T(8,128)(2,1)S(1)} %get-tuple-element.18), channel_id=1, source_target_pairs={{0,2},{2,4},{4,6},{1,3},{3,5},{5,7},{8,10},{10,12},{12,14},{9,11},... | collective-permute-start | bytes 49160 | tf_op jit(solution)/shard_map/ppermute | solution.py:18
  13.2 1.3 collective-permute-start.1
  15.2 4.5 %collective-permute-start.3 = (bf16[1,1,64,128]{3,2,1,0:T(8,128)(2,1)S(1)}, bf16[1,1,64,128]{3,2,1,0:T(8,128)(2,1)S(1)}, u32[]{:S(2)}, u32[]{:S(2)}) collective-permute-start(bf16[1,1,64,128]{3,2,1,0:T(8,128)(2,1)S(1)} %get-tuple-element.16), channel_id=1, source_target_pairs={{0,2},{2,4},{4,6},{1,3},{3,5},{5,7},{8,10},{10,12},{12,14},{9,11},... | collective-permute-start | bytes 49160 | tf_op jit(solution)/shard_map/ppermute | solution.py:18
  19.8 1.3 collective-permute-start.4
  22.5 1.3 collective-permute-start.2
  23.8 1.3 collective-permute-start.7
  25.5 2.9 collective-permute-start.5
  28.4 1.3 collective-permute-start.6
  34.5 112.6 %all-reduce.4.cloned.1.call-done = f32[294912]{0:T(1024)} async-done(((f32[294912]{0:T(1024)}), f32[294912]{0:T(1024)}) %all-reduce.4.cloned.1.call-update) | async-done | bytes 1179664 | tf_op jit(solution)/shard_map/psum | solution.py:59
  147.1 2.3 multiply_reduce_fusion
  150.2 53.1 %all-gather.2.cloned.1.call-done = f32[294912]{0:T(1024)} async-done(((f32[9216]{0:T(1024)}), f32[294912]{0:T(1024)}) %all-gather.2.cloned.1.call-update) | async-done | bytes 1179664 | tf_op jit(solution)/shard_map/all_gather | solution.py:60
  203.2 1.5 add_convert_fusion
  204.8 3.2 multiply_convert_fusion.1
  209.4 3.4 multiply_convert_fusion
  213.2 1.1 copy-done.4
  214.4 1.3 convolution_bitcast_fusion.13
  215.8 2.5 collective-permute-start.8
  218.4 1.6 collective-permute-start.9
  220.0 2.1 convolution_bitcast_fusion.4
  222.1 1.4 convolution_bitcast_fusion.11
  223.5 1.4 convolution_bitcast_fusion.9
  224.9 1.3 convolution_bitcast_fusion.10
  226.2 1.4 convolution_bitcast_fusion.14
  227.6 1.4 convolution_bitcast_fusion.12
  229.0 1.4 convolution_bitcast_fusion.17
  230.4 1.4 convolution_bitcast_fusion.15
  231.8 1.3 convolution_bitcast_fusion.16
  234.3 1.8 collective-permute-start.10
  236.1 1.3 collective-permute-start.11
  243.1 1.1 pad_maximum_fusion.1
  244.2 132.5 %all-reduce.6.cloned.1.call-done = f32[294912]{0:T(1024)} async-done(((f32[294912]{0:T(1024)}), f32[294912]{0:T(1024)}) %all-reduce.6.cloned.1.call-update) | async-done | bytes 1179664
  376.7 1.4 dynamic-slice
  (98 shorter events, 17.2 us)
Async XLA Ops:
  6.5 1.5 copy-start.3
  6.5 140.6 %all-reduce.4.cloned.1.call-start = ((), (), s32[]{:S(2)}) async-start(), calls=%async_computation.1 | async-start | bytes 2359296 | tf_op jit(solution)/shard_map/psum | solution.py:59
  7.3 196.0 %all-gather.2.cloned.1.call-start = ((), (), s32[]{:S(2)}) async-start(), calls=%async_computation | async-start | bytes 1216512 | tf_op jit(solution)/shard_map/all_gather | solution.py:60
  8.0 368.7 %all-reduce.6.cloned.1.call-start = ((), (), s32[]{:S(2)}) async-start(), calls=%async_computation.2 | async-start | bytes 2359296
  8.1 17.1 %copy-start.5 = (bf16[1,64,64,128]{3,2,1,0:T(8,128)(2,1)S(1)}, bf16[1,64,64,128]{3,2,1,0:T(8,128)(2,1)}, u32[]{:S(2)}) copy-start(bf16[1,64,64,128]{3,2,1,0:T(8,128)(2,1)} %param.5) | copy-start | bytes 3145732
  8.1 13.0 %collective-permute-start = (bf16[1,1,64,128]{3,2,1,0:T(8,128)(2,1)S(1)}, bf16[1,1,64,128]{3,2,1,0:T(8,128)(2,1)S(1)}, u32[]{:S(2)}, u32[]{:S(2)}) collective-permute-start(bf16[1,1,64,128]{3,2,1,0:T(8,128)(2,1)S(1)} %get-tuple-element.18), channel_id=1, source_target_pairs={{0,2},{2,4},{4,6},{1,3},{3,5},{5,7},{8,10},{10,12},{12,14},{9,11},... | collective-permute-start | bytes 49160 | tf_op jit(solution)/shard_map/ppermute | solution.py:18
  13.2 8.6 %collective-permute-start.1 = (bf16[1,1,64,128]{3,2,1,0:T(8,128)(2,1)S(1)}, bf16[1,1,64,128]{3,2,1,0:T(8,128)(2,1)S(1)}, u32[]{:S(2)}, u32[]{:S(2)}) collective-permute-start(bf16[1,1,64,128]{3,2,1,0:T(8,128)(2,1)S(1)} %get-tuple-element.17), channel_id=1, source_target_pairs={{2,0},{4,2},{6,4},{3,1},{5,3},{7,5},{10,8},{12,10},{14,12},{11,9},... | collective-permute-start | bytes 49160 | tf_op jit(solution)/shard_map/ppermute | solution.py:20
  15.2 9.9 %collective-permute-start.3 = (bf16[1,1,64,128]{3,2,1,0:T(8,128)(2,1)S(1)}, bf16[1,1,64,128]{3,2,1,0:T(8,128)(2,1)S(1)}, u32[]{:S(2)}, u32[]{:S(2)}) collective-permute-start(bf16[1,1,64,128]{3,2,1,0:T(8,128)(2,1)S(1)} %get-tuple-element.16), channel_id=1, source_target_pairs={{0,2},{2,4},{4,6},{1,3},{3,5},{5,7},{8,10},{10,12},{12,14},{9,11},... | collective-permute-start | bytes 49160 | tf_op jit(solution)/shard_map/ppermute | solution.py:18
  19.8 5.6 %collective-permute-start.4 = (bf16[1,1,64,128]{3,2,1,0:T(8,128)(2,1)S(1)}, bf16[1,1,64,128]{3,2,1,0:T(8,128)(2,1)S(1)}, u32[]{:S(2)}, u32[]{:S(2)}) collective-permute-start(bf16[1,1,64,128]{3,2,1,0:T(8,128)(2,1)S(1)} %get-tuple-element.15), channel_id=1, source_target_pairs={{2,0},{4,2},{6,4},{3,1},{5,3},{7,5},{10,8},{12,10},{14,12},{11,9},... | collective-permute-start | bytes 49160 | tf_op jit(solution)/shard_map/ppermute | solution.py:20
  21.1 0.6 copy-start.11
  21.8 0.6 copy-start.13
  22.5 7.2 %collective-permute-start.2 = (bf16[1,66,1,128]{3,2,1,0:T(2,128)(2,1)S(1)}, bf16[1,66,1,128]{3,2,1,0:T(2,128)(2,1)S(1)}, u32[]{:S(2)}, u32[]{:S(2)}) collective-permute-start(bf16[1,66,1,128]{3,2,1,0:T(2,128)(2,1)S(1)} %get-tuple-element.13), channel_id=1, source_target_pairs={{0,1},{2,3},{4,5},{6,7},{8,9},{10,11},{12,13},{14,15},{16,17},{18,... | collective-permute-start | bytes 50696 | tf_op jit(solution)/shard_map/ppermute | solution.py:18
  23.8 5.9 %collective-permute-start.7 = (bf16[1,66,1,128]{3,2,1,0:T(2,128)(2,1)S(1)}, bf16[1,66,1,128]{3,2,1,0:T(2,128)(2,1)S(1)}, u32[]{:S(2)}, u32[]{:S(2)}) collective-permute-start(bf16[1,66,1,128]{3,2,1,0:T(2,128)(2,1)S(1)} %get-tuple-element.14), channel_id=1, source_target_pairs={{1,0},{3,2},{5,4},{7,6},{9,8},{11,10},{13,12},{15,14},{17,16},{19,... | collective-permute-start | bytes 50696 | tf_op jit(solution)/shard_map/ppermute | solution.py:20
  25.5 6.1 %collective-permute-start.5 = (bf16[1,66,1,128]{3,2,1,0:T(2,128)(2,1)S(1)}, bf16[1,66,1,128]{3,2,1,0:T(2,128)(2,1)S(1)}, u32[]{:S(2)}, u32[]{:S(2)}) collective-permute-start(bf16[1,66,1,128]{3,2,1,0:T(2,128)(2,1)S(1)} %get-tuple-element.7), channel_id=1, source_target_pairs={{0,1},{2,3},{4,5},{6,7},{8,9},{10,11},{12,13},{14,15},{16,17},{18,... | collective-permute-start | bytes 50696 | tf_op jit(solution)/shard_map/ppermute | solution.py:18
  28.4 3.2 collective-permute-start.6
  32.7 1.0 copy-start.1
  147.1 56.1 %copy-start = (f32[294912]{0:T(1024)S(1)}, f32[294912]{0:T(1024)}, u32[]{:S(2)}) copy-start(f32[294912]{0:T(1024)} %all-reduce.4.cloned.1.call-done) | copy-start | bytes 3538948
  150.1 54.7 %copy-start.15 = (pred[8,9]{0,1:T(8,128)(4,1)S(1)}, pred[8,9]{0,1:T(8,128)(4,1)}, u32[]{:S(2)}) copy-start(pred[8,9]{0,1:T(8,128)(4,1)} %constant.21) | copy-start | bytes 220
  203.2 1.6 copy-start.9
  208.1 1.3 copy-start.2
  208.1 1.3 copy-start.10
  213.1 1.2 copy-start.4
  214.4 1.3 copy-start.7
  215.8 18.3 %collective-permute-start.8 = (bf16[1,1,64,128]{3,2,1,0:T(8,128)(2,1)S(1)}, bf16[1,1,64,128]{3,2,1,0:T(8,128)(2,1)S(1)}, u32[]{:S(2)}, u32[]{:S(2)}) collective-permute-start(bf16[1,1,64,128]{3,2,1,0:T(8,128)(2,1)S(1)} %slice.186), channel_id=1, source_target_pairs={{0,2},{2,4},{4,6},{1,3},{3,5},{5,7},{8,10},{10,12},{12,14},{9,11},... | collective-permute-start | bytes 49160 | tf_op jit(solution)/shard_map/ppermute | solution.py:18
  218.3 3.7 copy-start.8
  218.4 15.8 %collective-permute-start.9 = (bf16[1,1,64,128]{3,2,1,0:T(8,128)(2,1)S(1)}, bf16[1,1,64,128]{3,2,1,0:T(8,128)(2,1)S(1)}, u32[]{:S(2)}, u32[]{:S(2)}) collective-permute-start(bf16[1,1,64,128]{3,2,1,0:T(8,128)(2,1)S(1)} %slice.189), channel_id=1, source_target_pairs={{2,0},{4,2},{6,4},{3,1},{5,3},{7,5},{10,8},{12,10},{14,12},{11,9},... | collective-permute-start | bytes 49160 | tf_op jit(solution)/shard_map/ppermute | solution.py:20
  223.5 1.4 copy-start.14
  230.4 1.4 copy-start.12
  233.2 4.2 %copy-start.6 = (bf16[1,64,64,128]{3,2,1,0:T(8,128)(2,1)S(1)}, bf16[1,64,64,128]{3,2,1,0:T(8,128)(2,1)}, u32[]{:S(2)}) copy-start(bf16[1,64,64,128]{3,2,1,0:T(8,128)(2,1)} %param.5) | copy-start | bytes 3145732
  234.3 4.1 %collective-permute-start.10 = (bf16[1,66,1,128]{3,2,1,0:T(2,128)(2,1)S(1)}, bf16[1,66,1,128]{3,2,1,0:T(2,128)(2,1)S(1)}, u32[]{:S(2)}, u32[]{:S(2)}) collective-permute-start(bf16[1,66,1,128]{3,2,1,0:T(2,128)(2,1)S(1)} %get-tuple-element.11), channel_id=1, source_target_pairs={{0,1},{2,3},{4,5},{6,7},{8,9},{10,11},{12,13},{14,15},{16,17},{18,... | collective-permute-start | bytes 50696 | tf_op jit(solution)/shard_map/ppermute | solution.py:18
  236.1 3.1 collective-permute-start.11
Sparse Core Ops, SparseCore 0:
  12.7 134.3 all-reduce.3
  150.1 53.0 all-gather.1
  244.3 132.3 all-reduce.5
where the time goes:
time: 385 us
  waiting for transfers between devices  301 us (78%)
  starting transfers between devices  26.3 us (7%)
  matrix products  24.9 us (6%)
  between operations  14.5 us (4%)
  local copies, waits for them, and re-layouts  11.1 us (3%)
  other arithmetic  7.21 us (2%)
    unnamed x4, waiting for transfers between devices  134 us
    psum x1, waiting for transfers between devices, on_device(): totals = lax.psum(local_part, ('scene', 'row', 'col'))  113 us
    all_gather x1, waiting for transfers between devices, on_device(): lax.all_gather(params, ('scene', 'row', 'col'), axis=0, tiled=True)  53.1 us
    dot_general x18, matrix products, kernel_grad(): jnp.einsum('nhwc,nhwd->cd', window, errors, preferred_element_type=jnp.fl...  18.2 us
    ppermute x6, starting transfers between devices, with_halo(): lax.ppermute(tail, axis, [(i, (i + 1) % count) for i in range(ends)])  18.1 us
    ppermute x6, starting transfers between devices, with_halo(): lax.ppermute(head, axis, [((i + 1) % count, i) for i in range(ends)])  8.06 us
  transfers between devices with their start and end apart: 15, of which 5 were waited for; matrix products, arithmetic and copies ran while one was open for 6% of the time, Pallas kernels for 0%

commit v1 on v0

--- a/solution.py
+++ b/solution.py
@@ -1,10 +1,253 @@
+import functools
+
 import jax
 import jax.numpy as jnp
 from jax import lax
+from jax.experimental import pallas as pl
+from jax.experimental.pallas import tpu as pltpu
 from jax.sharding import PartitionSpec as P
 
 radius = 2.0
 epsilon = 1e-06
+AXES = ("scene", "row", "col")
+MESH = pl.DeviceIdType.MESH
+LANES = 128
+
+
+class Place:
+    def __init__(self, sizes):
+        self.scenes, self.rows, self.cols = sizes
+        self.pairs = self.cols // 2
+        self.n = self.scenes * self.rows * self.pairs
+        col = lax.axis_index("col")
+        self.half = lax.rem(col, 2)
+        self.me = (lax.axis_index("scene") * self.rows + lax.axis_index("row")) * self.pairs + col // 2
+
+    def device(self, chip, half):
+        return {
+            "scene": chip // (self.rows * self.pairs),
+            "row": lax.rem(chip // self.pairs, self.rows),
+            "col": lax.rem(chip, self.pairs) * 2 + half,
+        }
+
+    def after(self, step):
+        return lax.rem(self.me + step, self.n)
+
+    def before(self, step):
+        return lax.rem(self.me + self.n - step, self.n)
+
+
+def loop(low, high, body):
+    def wrapped(j, carry):
+        body(j)
+        return carry
+
+    lax.fori_loop(low, high, wrapped, 0)
+
+
+def wait_all(ref, sem):
+    pltpu.make_async_copy(ref, ref, sem).wait()
+
+
+def enter(place, everyone):
+    barrier = pltpu.get_barrier_semaphore()
+
+    def greet(j):
+        chip = place.after(j)
+        pl.semaphore_signal(barrier, inc=1, device_id=place.device(chip, place.half), device_id_type=MESH)
+        if everyone:
+            pl.semaphore_signal(barrier, inc=1, device_id=place.device(chip, 1 - place.half), device_id_type=MESH)
+
+    pl.semaphore_signal(barrier, inc=1, device_id=place.device(place.me, 1 - place.half), device_id_type=MESH)
+    loop(1, place.n, greet)
+    pl.semaphore_wait(barrier, (2 * place.n - 1) if everyone else place.n)
+
+
+def load_own(place, data, own, own_sem):
+    def start(j):
+        chip = place.after(j + 1)
+        pltpu.make_async_copy(data.at[chip, place.half], own.at[chip], own_sem.at[j]).start()
+
+    loop(0, place.n, start)
+
+
+def scatter_sum(place, data, own, theirs, sums, landed, own_sem, swap_send, swap_recv, peer_send, peer_recv):
+    n, me, half = place.n, place.me, place.half
+
+    def swap(j):
+        chip = place.after(j + 1)
+        return pltpu.make_async_remote_copy(
+            src_ref=data.at[chip, 1 - half],
+            dst_ref=theirs.at[chip],
+            send_sem=swap_send,
+            recv_sem=swap_recv.at[j],
+            device_id=place.device(me, 1 - half),
+            device_id_type=MESH,
+        )
+
+    loop(0, n, lambda j: swap(j).start())
+
+    def arrive(j):
+        chip = place.after(j + 1)
+        pltpu.make_async_copy(data.at[chip, half], own.at[chip], own_sem.at[j]).wait()
+        swap(j).wait_recv()
+
+    def pass_on(j):
+        chip = place.after(j + 1)
+        arrive(j)
+        sums[j] = (own[chip] + theirs[chip]).astype(sums.dtype)
+        pltpu.make_async_remote_copy(
+            src_ref=sums.at[j],
+            dst_ref=landed.at[j],
+            send_sem=peer_send,
+            recv_sem=peer_recv,
+            device_id=place.device(chip, half),
+            device_id_type=MESH,
+        ).start()
+
+    loop(0, n - 1, pass_on)
+    arrive(n - 1)
+    total = own[me] + theirs[me]
+    wait_all(landed, peer_recv)
+    total = lax.fori_loop(0, n - 1, lambda j, t: t + landed[j].astype(jnp.float32), total)
+    wait_all(theirs, swap_send)
+    wait_all(sums, peer_send)
+    return total
+
+
+def perturb_kernel(sizes, data, params, out, own, theirs, sums, landed, square, squares, mine,
+                   own_sem, swap_send, swap_recv, peer_send, peer_recv,
+                   sq_send, sq_recv, gather_send, gather_recv, relay_send, relay_recv):
+    place = Place(sizes)
+    n, me, half = place.n, place.me, place.half
+    load_own(place, data, own, own_sem)
+    enter(place, True)
+    grads = scatter_sum(place, data, own, theirs, sums, landed, own_sem, swap_send, swap_recv, peer_send, peer_recv)
+
+    local = jnp.sum(grads * grads)
+    square[...] = jnp.full(square.shape, local, jnp.float32)
+
+    def tell(chip, to_half, slot):
+        pltpu.make_async_remote_copy(
+            src_ref=square.at[0],
+            dst_ref=squares.at[slot],
+            send_sem=sq_send,
+            recv_sem=sq_recv,
+            device_id=place.device(chip, to_half),
+            device_id_type=MESH,
+        ).start()
+
+    def tell_chip(j):
+        chip = place.after(j)
+        tell(chip, half, 2 * j - 1)
+        tell(chip, 1 - half, 2 * j)
+
+    tell(me, 1 - half, 0)
+    loop(1, n, tell_chip)
+    wait_all(squares, sq_recv)
+    norm2 = square[0] + jnp.sum(squares[...], axis=0)
+    factor = radius / (jnp.sqrt(norm2) + epsilon)
+    mine[...] = (params[...] + factor * grads).astype(mine.dtype)
+    wait_all(squares, sq_send)
+
+    out[me, half] = mine[...]
+
+    def relay(chip, j):
+        return pltpu.make_async_remote_copy(
+            src_ref=out.at[chip, half],
+            dst_ref=out.at[chip, half],
+            send_sem=relay_send,
+            recv_sem=relay_recv,
+            device_id=place.device(me, 1 - half),
+            device_id_type=MESH,
+        )
+
+    def give(j):
+        return pltpu.make_async_remote_copy(
+            src_ref=mine,
+            dst_ref=out.at[me, half],
+            send_sem=gather_send,
+            recv_sem=gather_recv.at[j],
+            device_id=place.device(place.after(j + 1), half),
+            device_id_type=MESH,
+        )
+
+    loop(0, n - 1, lambda j: give(j).start())
+    pltpu.make_async_remote_copy(
+        src_ref=mine,
+        dst_ref=out.at[me, half],
+        send_sem=relay_send,
+        recv_sem=relay_recv,
+        device_id=place.device(me, 1 - half),
+        device_id_type=MESH,
+    ).start()
+
+    def pass_on(j):
+        give(j).wait_recv()
+        relay(place.before(j + 1), j).start()
+
+    loop(0, n - 1, pass_on)
+    wait_all(out.at[:, 0], relay_recv)
+    wait_all(out.at[:, 0], relay_send)
+    wait_all(landed, gather_send)
+
+
+def scatter_kernel(sizes, data, out, own, theirs, sums, landed,
+                   own_sem, swap_send, swap_recv, peer_send, peer_recv):
+    place = Place(sizes)
+    load_own(place, data, own, own_sem)
+    enter(place, False)
+    out[...] = scatter_sum(place, data, own, theirs, sums, landed, own_sem, swap_send, swap_recv, peer_send, peer_recv)
+
+
+def sum_scratch(n, rows):
+    dma = pltpu.SemaphoreType.DMA
+    buffers = [
+        pltpu.VMEM((n, rows, LANES), jnp.float32),
+        pltpu.VMEM((n, rows, LANES), jnp.float32),
+        pltpu.VMEM((n - 1, rows, LANES), jnp.bfloat16),
+        pltpu.VMEM((n - 1, rows, LANES), jnp.bfloat16),
+    ]
+    return buffers, [dma((n,)), dma, dma((n,)), dma, dma]
+
+
+def perturbed_params(sizes, local_part, share):
+    n = sizes[0] * sizes[1] * sizes[2] // 2
+    rows = share.size // LANES
+    dma = pltpu.SemaphoreType.DMA
+    buffers, sems = sum_scratch(n, rows)
+    return pl.pallas_call(
+        functools.partial(perturb_kernel, sizes),
+        out_shape=jax.ShapeDtypeStruct((n, 2, rows, LANES), jnp.bfloat16),
+        in_specs=[pl.BlockSpec(memory_space=pl.ANY), pl.BlockSpec(memory_space=pltpu.VMEM)],
+        out_specs=pl.BlockSpec(memory_space=pltpu.VMEM),
+        scratch_shapes=buffers
+        + [
+            pltpu.VMEM((1, 1, LANES), jnp.float32),
+            pltpu.VMEM((2 * n - 1, 1, LANES), jnp.float32),
+            pltpu.VMEM((rows, LANES), jnp.bfloat16),
+        ]
+        + sems
+        + [dma, dma, dma, dma((n,)), dma, dma],
+        compiler_params=pltpu.CompilerParams(collective_id=0, has_side_effects=True),
+        cost_estimate=pl.CostEstimate(flops=1000000, bytes_accessed=60000000, transcendentals=0),
+        name="perturb",
+    )(local_part.reshape(n, 2, rows, LANES), share.reshape(rows, LANES))
+
+
+def scattered_sum(sizes, local):
+    n = sizes[0] * sizes[1] * sizes[2] // 2
+    rows = local.size // (2 * n * LANES)
+    buffers, sems = sum_scratch(n, rows)
+    return pl.pallas_call(
+        functools.partial(scatter_kernel, sizes),
+        out_shape=jax.ShapeDtypeStruct((rows, LANES), jnp.float32),
+        in_specs=[pl.BlockSpec(memory_space=pl.ANY)],
+        out_specs=pl.BlockSpec(memory_space=pltpu.VMEM),
+        scratch_shapes=buffers + sems,
+        compiler_params=pltpu.CompilerParams(collective_id=1, has_side_effects=True),
+        name="scatter_sum",
+    )(local.reshape(n, 2, rows, LANES)).reshape(-1)
 
 
 def with_halo(cells, sides, width):
@@ -54,12 +297,8 @@
     return jnp.stack(rows_out)
 
 
-def on_device(scenes, cotangent, params, partials):
-    local_part = partials[0]
-    totals = lax.psum(local_part, ("scene", "row", "col"))
-    raw_whole = lax.all_gather(params, ("scene", "row", "col"), axis=0, tiled=True)
-    factor = radius / (jnp.sqrt(jnp.sum(totals * totals)) + epsilon)
-    whole = (raw_whole + factor * totals).astype(jnp.bfloat16)
+def on_device(sizes, scenes, cotangent, params, partials):
+    whole = perturbed_params(sizes, partials[0], params)
     channels = scenes.shape[3]
     kernels = whole.reshape(2, 3, 3, channels, channels)
     kernel_one = kernels[0]
@@ -72,20 +311,21 @@
     delta = (back * squash * (1.0 + pre * (1.0 - squash))).astype(jnp.bfloat16)
     grad_one = kernel_grad(padded_in, delta)
     grad_two = kernel_grad(widened(hidden), cotangent)
-    local_grad = jnp.stack([grad_one, grad_two]).reshape(-1)
-    return lax.psum_scatter(local_grad, ("scene", "row", "col"), scatter_dimension=0, tiled=True)
+    local_grad = jnp.stack([grad_one, grad_two])
+    return scattered_sum(sizes, local_grad)
 
 
 def solution(mesh):
+    sizes = tuple(mesh.shape[axis] for axis in AXES)
     return jax.shard_map(
-        on_device,
+        functools.partial(on_device, sizes),
         mesh=mesh,
         in_specs=(
             P("scene", "row", "col", None),
             P("scene", "row", "col", None),
-            P(("scene", "row", "col")),
-            P(("scene", "row", "col"), None),
+            P(AXES),
+            P(AXES, None),
         ),
-        out_specs=P(("scene", "row", "col")),
+        out_specs=P(AXES),
         check_vma=False,
     )

time: 385 us -> 177 us (0.46)
  waiting for transfers between devices: 301 us -> 4.66 us
  Pallas kernels: 0 us -> 46.5 us
  other arithmetic: 7.21 us -> 38.4 us
  between operations: 14.5 us -> 0.49 us
  local copies, waits for them, and re-layouts: 11.1 us -> 22.6 us
  matrix products: 24.9 us -> 36.2 us
    unnamed x4 -> x0, waiting for transfers between devices: 134 us -> none
    psum x1 -> x0, waiting for transfers between devices: 113 us -> none  [on_device(): totals = lax.psum(local_part, ('scene', 'row', 'col'))]
    all_gather x1 -> x0, waiting for transfers between devices: 53.1 us -> none  [on_device(): lax.all_gather(params, ('scene', 'row', 'col'), axis=0, tiled=True)]
    pallas_call x0 -> x2, Pallas kernels: none -> 46.5 us  [the longest x1 32.2 us: perturbed_params(): pl.pallas_call(functools.partial(perturb_kernel, sizes), out_shape=jax.Sh...]
    concatenate x3, other arithmetic: 2.08 us -> 36.9 us  [with_halo(): jnp.concatenate([lax.ppermute(tail, axis, [(i, (i + 1) % count) for i in...]
    conv_general_dilated x2, matrix products: 6.66 us -> 27.2 us  [convolve(): lax.conv_general_dilated(padded, kernel, (1, 1), 'VALID', dimension_numbe...]
    slice x0 -> x1, local copies, waits for them, and re-layouts: none -> 13.1 us  [kernel_grad(): window = padded[:, row_off:row_off + height, col_off:col_off + width, :]]
    dot_general x18, matrix products: 18.2 us -> 8.99 us  [kernel_grad(): jnp.einsum('nhwc,nhwd->cd', window, errors, preferred_element_type=jnp.fl...]
  transfers between devices with their start and end apart: 15 -> 12, of which waited for: 5 -> 2; matrix products, arithmetic and copies ran while one was open for 6% -> 16% of each run, Pallas kernels for 0% -> 18%
where the time goes in v1:
time: 177 us; the launch traced here: 176 us
  Pallas kernels  46.5 us (26%)
  other arithmetic  38.4 us (22%)
  matrix products  36.2 us (20%)
  starting transfers between devices  27.3 us (15%)
  local copies, waits for them, and re-layouts  22.6 us (13%)
  waiting for transfers between devices  4.66 us (3%)
    concatenate x3, other arithmetic, with_halo(): jnp.concatenate([lax.ppermute(tail, axis, [(i, (i + 1) % count) for i in...  36.9 us
    pallas_call x1, Pallas kernels, perturbed_params(): pl.pallas_call(functools.partial(perturb_kernel, sizes), out_shape=jax.Sh...  32.2 us
    conv_general_dilated x2, matrix products, convolve(): lax.conv_general_dilated(padded, kernel, (1, 1), 'VALID', dimension_numbe...  27.2 us
    ppermute x6, starting transfers between devices, with_halo(): lax.ppermute(tail, axis, [(i, (i + 1) % count) for i in range(ends)])  19.3 us
    pallas_call x1, Pallas kernels, scattered_sum(): pl.pallas_call(functools.partial(scatter_kernel, sizes), out_shape=jax.Sh...  14.3 us
    slice x1, local copies, waits for them, and re-layouts, kernel_grad(): window = padded[:, row_off:row_off + height, col_off:col_off + width, :]  13.1 us
    dot_general x18, matrix products, kernel_grad(): jnp.einsum('nhwc,nhwd->cd', window, errors, preferred_element_type=jnp.fl...  8.99 us
    ppermute x6, starting transfers between devices, with_halo(): lax.ppermute(head, axis, [((i + 1) % count, i) for i in range(ends)])  7.93 us
  transfers between devices with their start and end apart: 12, of which 2 were waited for; matrix products, arithmetic and copies ran while one was open for 16% of the time, Pallas kernels for 18%

profile of v1, /device:TPU:0, one launch (start us, length us, event | category | flops | bytes accessed | tf_op | source)
XLA Modules:
  0.0 176.0 jit_solution(12808258099455797463)
XLA Ops:
  0.0 0.8 fusion.75
  0.9 5.0 %collective-permute-start = (bf16[1,1,64,128]{3,0,2,1:T(2,128)(2,1)S(1)}, bf16[1,1,64,128]{3,0,2,1:T(2,128)(2,1)S(1)}, u32[]{:S(2)}, u32[]{:S(2)}) collective-permute-start(bf16[1,1,64,128]{3,0,2,1:T(2,128)(2,1)S(1)} %copy.99), channel_id=1, source_target_pairs={{0,2},{2,4},{4,6},{1,3},{3,5},{5,7},{8,10},{10,12},{12,14},{9,11},... | collective-permute-start | bytes 49160 | tf_op jit(solution)/shard_map/ppermute | solution.py:261
  5.9 1.3 collective-permute-start.1
  7.2 0.7 fusion.74
  7.9 4.5 %collective-permute-start.3 = (bf16[1,1,64,128]{3,0,2,1:T(2,128)(2,1)S(1)}, bf16[1,1,64,128]{3,0,2,1:T(2,128)(2,1)S(1)}, u32[]{:S(2)}, u32[]{:S(2)}) collective-permute-start(bf16[1,1,64,128]{3,0,2,1:T(2,128)(2,1)S(1)} %copy.101), channel_id=1, source_target_pairs={{0,2},{2,4},{4,6},{1,3},{3,5},{5,7},{8,10},{10,12},{12,14},{9,11},... | collective-permute-start | bytes 49160 | tf_op jit(solution)/shard_map/ppermute | solution.py:261
  12.5 1.3 collective-permute-start.4
  13.8 32.2 %perturb.1 = bf16[16,2,72,128]{3,2,1,0:T(8,128)(2,1)} custom-call(f32[16,2,72,128]{3,2,1,0:T(8,128)} %bitcast.174, f32[72,128]{1,0:T(8,128)} %bitcast.178), custom_call_target="tpu_custom_call" | custom-call | flops 1000000 | bytes 60000000 | tf_op jit(solution)/shard_map/perturb/pallas_call | solution.py:219
  46.0 1.2 fusion.76
  47.3 2.3 %constant_dynamic-update-slice_fusion.1 = bf16[1,66,64,128]{3,0,2,1:T(2,128)(2,1)S(1)} fusion(bf16[1,66,64,128]{3,0,2,1:T(2,128)(2,1)S(1)} %constant_dynamic-update-slice_fusion.2, bf16[1,64,64,128]{3,2,1,0:T(8,128)(2,1)S(1)} %copy-done), kind=kLoop, calls=%fused_computation.111 | loop fusion | bytes 3145728
  49.8 2.3 %collective-permute-start.2 = (bf16[1,66,1,128]{3,0,2,1:T(2,128)(2,1)S(1)}, bf16[1,66,1,128]{3,0,2,1:T(2,128)(2,1)S(1)}, u32[]{:S(2)}, u32[]{:S(2)}) collective-permute-start(bf16[1,66,1,128]{3,0,2,1:T(2,128)(2,1)S(1)} %get-tuple-element.28), channel_id=1, source_target_pairs={{0,1},{2,3},{4,5},{6,7},{8,9},{10,11},{12,13},{14,15},{16,17},{18,... | collective-permute-start | bytes 50696 | tf_op jit(solution)/shard_map/ppermute | solution.py:261
  52.0 1.3 collective-permute-start.7
  53.4 2.3 %constant_dynamic-update-slice_fusion.4 = bf16[1,66,64,128]{3,0,2,1:T(2,128)(2,1)S(1)} fusion(bf16[1,66,64,128]{3,0,2,1:T(2,128)(2,1)S(1)} %constant_dynamic-update-slice_fusion.5, bf16[1,64,64,128]{3,2,1,0:T(8,128)(2,1)S(1)} %copy-done.1), kind=kLoop, calls=%fused_computation.114 | loop fusion | bytes 3145728
  55.9 3.0 %collective-permute-start.5 = (bf16[1,66,1,128]{3,0,2,1:T(2,128)(2,1)S(1)}, bf16[1,66,1,128]{3,0,2,1:T(2,128)(2,1)S(1)}, u32[]{:S(2)}, u32[]{:S(2)}) collective-permute-start(bf16[1,66,1,128]{3,0,2,1:T(2,128)(2,1)S(1)} %get-tuple-element.22), channel_id=1, source_target_pairs={{0,1},{2,3},{4,5},{6,7},{8,9},{10,11},{12,13},{14,15},{16,17},{18,... | collective-permute-start | bytes 50696 | tf_op jit(solution)/shard_map/ppermute | solution.py:261
  58.9 1.5 collective-permute-start.6
  60.4 13.5 %multiply_convert_fusion = (bf16[1,64,64,128]{3,0,2,1:T(2,128)(2,1)S(1)}, f32[1,64,64,128]{3,0,2,1:T(1,128)S(1)}, f32[1,64,64,128]{3,0,2,1:T(1,128)S(1)}) fusion(bf16[3,3,128,128]{3,2,1,0:T(8,128)(2,1)S(1)} %bitcast.176, bf16[1,66,1,128]{3,0,2,1:T(2,128)(2,1)S(1)} %collective-permute-done.7, ...), kind=kOutput, calls=%fused_computation.23 | convolution fusion | flops 1213926400 | bytes 6652928 | tf_op jit(solution)/shard_map/conv_general_dilated | solution.py:271
  74.5 13.7 %fusion.1 = bf16[1,64,64,128]{3,0,2,1:T(2,128)(2,1)S(1)} fusion(f32[1,64,64,128]{3,0,2,1:T(1,128)S(1)} %get-tuple-element.6, bf16[3,3,128,128]{3,2,1,0:T(8,128)(2,1)S(1)} %bitcast.175, bf16[1,66,1,128]{3,0,2,1:T(2,128)(2,1)S(1)} %collective-permute-done.6, bf16[1,66,64,128]{3,0,2,1:T(2,128)(2,1)S(1)} %constant_dynamic-update-slice_fusion.3, ...), kind=kOutput, calls=%fused_computation.2 | convolution fusion | flops 1214450688 | bytes 6652928 | tf_op jit(solution)/shard_map/conv_general_dilated | solution.py:271
  88.9 17.7 %fusion.9 = (bf16[1,64,64,128]{3,0,2,1:T(2,128)(2,1)S(1)}, bf16[1,64,64,128]{3,0,2,1:T(2,128)(2,1)S(1)}, bf16[1,64,64,128]{3,0,2,1:T(2,128)(2,1)S(1)}, bf16[1,64...) fusion(bf16[1,66,1,128]{3,0,2,1:T(2,128)(2,1)S(1)} %collective-permute-don, ...), kind=kLoop, calls=%fused_computation.18 | loop fusion | flops 3145728 | bytes 7406592 | tf_op jit(solution)/shard_map/concatenate | solution.py:259
  108.7 0.5 convolution_bitcast_fusion.16
  110.7 2.6 %collective-permute-start.8 = (bf16[1,1,64,128]{3,0,2,1:T(2,128)(2,1)S(1)}, bf16[1,1,64,128]{3,0,2,1:T(2,128)(2,1)S(1)}, u32[]{:S(2)}, u32[]{:S(2)}) collective-permute-start(bf16[1,1,64,128]{3,0,2,1:T(2,128)(2,1)S(1)} %get-tuple-element.32), channel_id=1, source_target_pairs={{0,2},{2,4},{4,6},{1,3},{3,5},{5,7},{8,10},{10,12},{12,14},{9,11},... | collective-permute-start | bytes 49160 | tf_op jit(solution)/shard_map/ppermute | solution.py:261
  113.4 1.3 collective-permute-start.9
  115.0 4.4 %collective-permute-done.9 = bf16[1,1,64,128]{3,0,2,1:T(2,128)(2,1)S(1)} collective-permute-done((bf16[1,1,64,128]{3,0,2,1:T(2,128)(2,1)S(1)}, bf16[1,1,64,128]{3,0,2,1:T(2,128)(2,1)S(1)}, u32[]{:S(2)}, u32[]{:S(2)}) %collective-permute-start.9) | collective-permute-done | bytes 16416 | tf_op jit(solution)/shard_map/ppermute | solution.py:263
  119.5 1.9 %collective-permute-start.10 = (bf16[1,66,1,128]{3,0,2,1:T(2,128)(2,1)S(1)}, bf16[1,66,1,128]{3,0,2,1:T(2,128)(2,1)S(1)}, u32[]{:S(2)}, u32[]{:S(2)}) collective-permute-start(bf16[1,66,1,128]{3,0,2,1:T(2,128)(2,1)S(1)} %get-tuple-element.26), channel_id=1, source_target_pairs={{0,1},{2,3},{4,5},{6,7},{8,9},{10,11},{12,13},{14,15},{16,17},{18,... | collective-permute-start | bytes 50696 | tf_op jit(solution)/shard_map/ppermute | solution.py:261
  121.4 1.3 collective-permute-start.11
  122.7 5.8 %pad_maximum_fusion.6 = (bf16[1,64,64,128]{3,0,2,1:T(2,128)(2,1)S(1)}, bf16[1,64,64,128]{3,0,2,1:T(2,128)(2,1)S(1)}) fusion(bf16[1,64,64,128]{3,0,2,1:T(2,128)(2,1)S(1)} %get-tuple-element.5, bf16[1,1,64,128]{3,0,2,1:T(2,128)(2,1)S(1)} %collective-permute-done.8, bf16[1,1,64,128]{3,0,2,1:T(2,128)(2,1)S(1)} %collective-permute-done.9), kind=kLoop, calls=%fused_computation.20 | loop fusion | flops 1048576 | bytes 3178496 | tf_op jit(solution)/shard_map/concatenate | solution.py:259
  129.5 13.4 %maximum_maximum_fusion = (bf16[1,66,65,128]{3,0,2,1:T(2,128)(2,1)S(1)}, bf16[1,66,65,128]{3,0,2,1:T(2,128)(2,1)S(1)}) fusion(bf16[1,1,64,128]{3,0,2,1:T(2,128)(2,1)S(1)} %collective-permute-done.9, bf16[1,64,64,128]{3,0,2,1:T(2,128)(2,1)S(1)} %get-tuple-element.5, bf16[1,1,64,128]{3,0,2,1:T(2,128)(2,1)S(1)} %collective-permute-done.8, ...), kind=kLoop, calls=%fused_computation.13 | loop fusion | flops 3294720 | bytes 3311616 | tf_op jit(solution)/shard_map/concatenate | solution.py:259
  143.0 13.1 %fusion.69 = (bf16[1,64,64,128]{3,0,2,1:T(2,128)(2,1)S(1)}, bf16[1,64,64,128]{3,0,2,1:T(2,128)(2,1)S(1)}, bf16[1,64,64,128]{3,0,2,1:T(2,128)(2,1)S(1)}, bf16[1,6...) fusion(bf16[1,66,65,128]{3,0,2,1:T(2,128)(2,1)S(1)} %get-tuple-element.2, ...), kind=kLoop, calls=%fused_computation.120 | loop fusion | bytes 12582912 | tf_op jit(solution)/shard_map/slice | solution.py:292
  156.6 0.5 convolution_bitcast_fusion.8
  157.1 0.5 convolution_bitcast_fusion.3
  158.1 0.5 convolution_bitcast_fusion
  159.2 1.2 pad_maximum_fusion.9
  160.4 14.3 %scatter_sum.1 = f32[72,128]{1,0:T(8,128)} custom-call(f32[16,2,72,128]{3,2,1,0:T(8,128)} %bitcast.173), custom_call_target="tpu_custom_call" | custom-call | tf_op jit(solution)/shard_map/scatter_sum/pallas_call | solution.py:242
  174.6 1.4 copy.108
  (51 shorter events, 8.2 us)
Async XLA Ops:
  0.0 47.3 %copy-start = (bf16[1,64,64,128]{3,2,1,0:T(8,128)(2,1)S(1)}, bf16[1,64,64,128]{3,2,1,0:T(8,128)(2,1)}, u32[]{:S(2)}) copy-start(bf16[1,64,64,128]{3,2,1,0:T(8,128)(2,1)} %param.4) | copy-start | bytes 3145732
  0.9 46.4 %collective-permute-start = (bf16[1,1,64,128]{3,0,2,1:T(2,128)(2,1)S(1)}, bf16[1,1,64,128]{3,0,2,1:T(2,128)(2,1)S(1)}, u32[]{:S(2)}, u32[]{:S(2)}) collective-permute-start(bf16[1,1,64,128]{3,0,2,1:T(2,128)(2,1)S(1)} %copy.99), channel_id=1, source_target_pairs={{0,2},{2,4},{4,6},{1,3},{3,5},{5,7},{8,10},{10,12},{12,14},{9,11},... | collective-permute-start | bytes 49160 | tf_op jit(solution)/shard_map/ppermute | solution.py:261
  5.9 43.8 %collective-permute-start.1 = (bf16[1,1,64,128]{3,0,2,1:T(2,128)(2,1)S(1)}, bf16[1,1,64,128]{3,0,2,1:T(2,128)(2,1)S(1)}, u32[]{:S(2)}, u32[]{:S(2)}) collective-permute-start(bf16[1,1,64,128]{3,0,2,1:T(2,128)(2,1)S(1)} %copy.100), channel_id=1, source_target_pairs={{2,0},{4,2},{6,4},{3,1},{5,3},{7,5},{10,8},{12,10},{14,12},{11,9},... | collective-permute-start | bytes 49160 | tf_op jit(solution)/shard_map/ppermute | solution.py:263
  7.9 45.4 %collective-permute-start.3 = (bf16[1,1,64,128]{3,0,2,1:T(2,128)(2,1)S(1)}, bf16[1,1,64,128]{3,0,2,1:T(2,128)(2,1)S(1)}, u32[]{:S(2)}, u32[]{:S(2)}) collective-permute-start(bf16[1,1,64,128]{3,0,2,1:T(2,128)(2,1)S(1)} %copy.101), channel_id=1, source_target_pairs={{0,2},{2,4},{4,6},{1,3},{3,5},{5,7},{8,10},{10,12},{12,14},{9,11},... | collective-permute-start | bytes 49160 | tf_op jit(solution)/shard_map/ppermute | solution.py:261
  12.5 43.2 %collective-permute-start.4 = (bf16[1,1,64,128]{3,0,2,1:T(2,128)(2,1)S(1)}, bf16[1,1,64,128]{3,0,2,1:T(2,128)(2,1)S(1)}, u32[]{:S(2)}, u32[]{:S(2)}) collective-permute-start(bf16[1,1,64,128]{3,0,2,1:T(2,128)(2,1)S(1)} %copy.102), channel_id=1, source_target_pairs={{2,0},{4,2},{6,4},{3,1},{5,3},{7,5},{10,8},{12,10},{14,12},{11,9},... | collective-permute-start | bytes 49160 | tf_op jit(solution)/shard_map/ppermute | solution.py:263
  46.0 7.3 %copy-start.1 = (bf16[1,64,64,128]{3,2,1,0:T(8,128)(2,1)S(1)}, bf16[1,64,64,128]{3,2,1,0:T(8,128)(2,1)}, u32[]{:S(2)}) copy-start(bf16[1,64,64,128]{3,2,1,0:T(8,128)(2,1)} %param.5) | copy-start | bytes 3145732
  49.8 10.6 %collective-permute-start.2 = (bf16[1,66,1,128]{3,0,2,1:T(2,128)(2,1)S(1)}, bf16[1,66,1,128]{3,0,2,1:T(2,128)(2,1)S(1)}, u32[]{:S(2)}, u32[]{:S(2)}) collective-permute-start(bf16[1,66,1,128]{3,0,2,1:T(2,128)(2,1)S(1)} %get-tuple-element.28), channel_id=1, source_target_pairs={{0,1},{2,3},{4,5},{6,7},{8,9},{10,11},{12,13},{14,15},{16,17},{18,... | collective-permute-start | bytes 50696 | tf_op jit(solution)/shard_map/ppermute | solution.py:261
  52.0 8.4 %collective-permute-start.7 = (bf16[1,66,1,128]{3,0,2,1:T(2,128)(2,1)S(1)}, bf16[1,66,1,128]{3,0,2,1:T(2,128)(2,1)S(1)}, u32[]{:S(2)}, u32[]{:S(2)}) collective-permute-start(bf16[1,66,1,128]{3,0,2,1:T(2,128)(2,1)S(1)} %get-tuple-element.29), channel_id=1, source_target_pairs={{1,0},{3,2},{5,4},{7,6},{9,8},{11,10},{13,12},{15,14},{17,16},{19,... | collective-permute-start | bytes 50696 | tf_op jit(solution)/shard_map/ppermute | solution.py:263
  55.9 18.7 %collective-permute-start.5 = (bf16[1,66,1,128]{3,0,2,1:T(2,128)(2,1)S(1)}, bf16[1,66,1,128]{3,0,2,1:T(2,128)(2,1)S(1)}, u32[]{:S(2)}, u32[]{:S(2)}) collective-permute-start(bf16[1,66,1,128]{3,0,2,1:T(2,128)(2,1)S(1)} %get-tuple-element.22), channel_id=1, source_target_pairs={{0,1},{2,3},{4,5},{6,7},{8,9},{10,11},{12,13},{14,15},{16,17},{18,... | collective-permute-start | bytes 50696 | tf_op jit(solution)/shard_map/ppermute | solution.py:261
  58.9 15.6 %collective-permute-start.6 = (bf16[1,66,1,128]{3,0,2,1:T(2,128)(2,1)S(1)}, bf16[1,66,1,128]{3,0,2,1:T(2,128)(2,1)S(1)}, u32[]{:S(2)}, u32[]{:S(2)}) collective-permute-start(bf16[1,66,1,128]{3,0,2,1:T(2,128)(2,1)S(1)} %get-tuple-element.23), channel_id=1, source_target_pairs={{1,0},{3,2},{5,4},{7,6},{9,8},{11,10},{13,12},{15,14},{17,16},{19,... | collective-permute-start | bytes 50696 | tf_op jit(solution)/shard_map/ppermute | solution.py:263
  110.7 4.2 %collective-permute-start.8 = (bf16[1,1,64,128]{3,0,2,1:T(2,128)(2,1)S(1)}, bf16[1,1,64,128]{3,0,2,1:T(2,128)(2,1)S(1)}, u32[]{:S(2)}, u32[]{:S(2)}) collective-permute-start(bf16[1,1,64,128]{3,0,2,1:T(2,128)(2,1)S(1)} %get-tuple-element.32), channel_id=1, source_target_pairs={{0,2},{2,4},{4,6},{1,3},{3,5},{5,7},{8,10},{10,12},{12,14},{9,11},... | collective-permute-start | bytes 49160 | tf_op jit(solution)/shard_map/ppermute | solution.py:261
  113.4 6.0 %collective-permute-start.9 = (bf16[1,1,64,128]{3,0,2,1:T(2,128)(2,1)S(1)}, bf16[1,1,64,128]{3,0,2,1:T(2,128)(2,1)S(1)}, u32[]{:S(2)}, u32[]{:S(2)}) collective-permute-start(bf16[1,1,64,128]{3,0,2,1:T(2,128)(2,1)S(1)} %get-tuple-element.33), channel_id=1, source_target_pairs={{2,0},{4,2},{6,4},{3,1},{5,3},{7,5},{10,8},{12,10},{14,12},{11,9},... | collective-permute-start | bytes 49160 | tf_op jit(solution)/shard_map/ppermute | solution.py:263
  119.5 10.0 %collective-permute-start.10 = (bf16[1,66,1,128]{3,0,2,1:T(2,128)(2,1)S(1)}, bf16[1,66,1,128]{3,0,2,1:T(2,128)(2,1)S(1)}, u32[]{:S(2)}, u32[]{:S(2)}) collective-permute-start(bf16[1,66,1,128]{3,0,2,1:T(2,128)(2,1)S(1)} %get-tuple-element.26), channel_id=1, source_target_pairs={{0,1},{2,3},{4,5},{6,7},{8,9},{10,11},{12,13},{14,15},{16,17},{18,... | collective-permute-start | bytes 50696 | tf_op jit(solution)/shard_map/ppermute | solution.py:261
  121.4 8.1 %collective-permute-start.11 = (bf16[1,66,1,128]{3,0,2,1:T(2,128)(2,1)S(1)}, bf16[1,66,1,128]{3,0,2,1:T(2,128)(2,1)S(1)}, u32[]{:S(2)}, u32[]{:S(2)}) collective-permute-start(bf16[1,66,1,128]{3,0,2,1:T(2,128)(2,1)S(1)} %get-tuple-element.27), channel_id=1, source_target_pairs={{1,0},{3,2},{5,4},{7,6},{9,8},{11,10},{13,12},{15,14},{17,16},{19,... | collective-permute-start | bytes 50696 | tf_op jit(solution)/shard_map/ppermute | solution.py:263

commit v2 on v1

--- a/solution.py
+++ b/solution.py
@@ -115,13 +115,40 @@
     return total
 
 
-def perturb_kernel(sizes, data, params, out, own, theirs, sums, landed, square, squares, mine,
+AROUND = tuple((dr, dc) for dr in (-1, 0, 1) for dc in (-1, 0, 1) if dr or dc)
+
+
+def edge_of(dr, dc):
+    if dr:
+        return 1 if dr < 0 else 0
+    return 3 if dc < 0 else 2
+
+
+def start_halo(sizes, edges, halo, halo_send, halo_recv):
+    row, col = lax.axis_index("row"), lax.axis_index("col")
+    for slot, (dr, dc) in enumerate(AROUND):
+        pltpu.make_async_remote_copy(
+            src_ref=edges.at[edge_of(dr, dc)],
+            dst_ref=halo.at[slot],
+            send_sem=halo_send,
+            recv_sem=halo_recv,
+            device_id={
+                "scene": lax.axis_index("scene"),
+                "row": lax.rem(row + sizes[1] - dr, sizes[1]),
+                "col": lax.rem(col + sizes[2] - dc, sizes[2]),
+            },
+            device_id_type=MESH,
+        ).start()
+
+
+def perturb_kernel(sizes, data, params, edges, out, halo, own, theirs, sums, landed, square, squares, mine,
                    own_sem, swap_send, swap_recv, peer_send, peer_recv,
-                   sq_send, sq_recv, gather_send, gather_recv, relay_send, relay_recv):
+                   sq_send, sq_recv, gather_send, gather_recv, relay_send, relay_recv, halo_send, halo_recv):
     place = Place(sizes)
     n, me, half = place.n, place.me, place.half
     load_own(place, data, own, own_sem)
     enter(place, True)
+    start_halo(sizes, edges, halo, halo_send, halo_recv)
     grads = scatter_sum(place, data, own, theirs, sums, landed, own_sem, swap_send, swap_recv, peer_send, peer_recv)
 
     local = jnp.sum(grads * grads)
@@ -190,6 +217,8 @@
     wait_all(out.at[:, 0], relay_recv)
     wait_all(out.at[:, 0], relay_send)
     wait_all(landed, gather_send)
+    wait_all(halo, halo_recv)
+    wait_all(halo, halo_send)
 
 
 def scatter_kernel(sizes, data, out, own, theirs, sums, landed,
@@ -211,16 +240,19 @@
     return buffers, [dma((n,)), dma, dma((n,)), dma, dma]
 
 
-def perturbed_params(sizes, local_part, share):
+def perturbed_params(sizes, local_part, share, edges):
     n = sizes[0] * sizes[1] * sizes[2] // 2
     rows = share.size // LANES
     dma = pltpu.SemaphoreType.DMA
     buffers, sems = sum_scratch(n, rows)
     return pl.pallas_call(
         functools.partial(perturb_kernel, sizes),
-        out_shape=jax.ShapeDtypeStruct((n, 2, rows, LANES), jnp.bfloat16),
-        in_specs=[pl.BlockSpec(memory_space=pl.ANY), pl.BlockSpec(memory_space=pltpu.VMEM)],
-        out_specs=pl.BlockSpec(memory_space=pltpu.VMEM),
+        out_shape=(
+            jax.ShapeDtypeStruct((n, 2, rows, LANES), jnp.bfloat16),
+            jax.ShapeDtypeStruct((len(AROUND),) + edges.shape[1:], edges.dtype),
+        ),
+        in_specs=[pl.BlockSpec(memory_space=pl.ANY)] + [pl.BlockSpec(memory_space=pltpu.VMEM)] * 2,
+        out_specs=(pl.BlockSpec(memory_space=pltpu.VMEM),) * 2,
         scratch_shapes=buffers
         + [
             pltpu.VMEM((1, 1, LANES), jnp.float32),
@@ -228,11 +260,11 @@
             pltpu.VMEM((rows, LANES), jnp.bfloat16),
         ]
         + sems
-        + [dma, dma, dma, dma((n,)), dma, dma],
+        + [dma, dma, dma, dma((n,)), dma, dma, dma, dma],
         compiler_params=pltpu.CompilerParams(collective_id=0, has_side_effects=True),
         cost_estimate=pl.CostEstimate(flops=1000000, bytes_accessed=60000000, transcendentals=0),
         name="perturb",
-    )(local_part.reshape(n, 2, rows, LANES), share.reshape(rows, LANES))
+    )(local_part.reshape(n, 2, rows, LANES), share.reshape(rows, LANES), edges)
 
 
 def scattered_sum(sizes, local):
@@ -250,69 +282,111 @@
     )(local.reshape(n, 2, rows, LANES)).reshape(-1)
 
 
-def with_halo(cells, sides, width):
-    for axis, dim in sides:
-        count = lax.axis_size(axis)
-        ends = count - 1
-        head = lax.slice_in_dim(cells, 0, width, axis=dim)
-        tail = lax.slice_in_dim(cells, cells.shape[dim] - width, cells.shape[dim], axis=dim)
-        cells = jnp.concatenate(
-            [
-                lax.ppermute(tail, axis, [(i, (i + 1) % count) for i in range(ends)]),
-                cells,
-                lax.ppermute(head, axis, [((i + 1) % count, i) for i in range(ends)]),
-            ],
-            axis=dim,
-        )
-    return cells
-
-
-def convolve(padded, kernel):
-    return lax.conv_general_dilated(
-        padded,
-        kernel,
-        (1, 1),
-        "VALID",
-        dimension_numbers=("NHWC", "HWIO", "NHWC"),
-        preferred_element_type=jnp.float32,
+def fill(sizes, which, cells, halo, cat, cols):
+    height, width, channels = cells.shape
+    row, col = lax.axis_index("row"), lax.axis_index("col")
+    inside_row = {-1: row > 0, 0: row >= 0, 1: row < sizes[1] - 1}
+    inside_col = {-1: col > 0, 0: col >= 0, 1: col < sizes[2] - 1}
+
+    def arrived(dr, dc):
+        inside = jnp.logical_and(inside_row[dr], inside_col[dc])
+        block = halo[AROUND.index((dr, dc)), which].astype(jnp.float32)
+        return jnp.where(inside, block, 0.0)
+
+    position = lax.broadcasted_iota(jnp.int32, (width, channels), 0)
+
+    def put(r, line, left, right):
+        before = jnp.where(position == 0, left, pltpu.roll(line, 1, 0))
+        behind = jnp.where(position == width - 1, right, pltpu.roll(line, width - 1, 0))
+        cat[r, :, 0:channels] = before.astype(cat.dtype)
+        cat[r, :, channels : 2 * channels] = line.astype(cat.dtype)
+        cat[r, :, 2 * channels : 3 * channels] = behind.astype(cat.dtype)
+
+    cols[0] = arrived(0, -1)
+    cols[1] = arrived(0, 1)
+    for dr, r in ((-1, 0), (1, height + 1)):
+        put(r, arrived(dr, 0), arrived(dr, -1)[width - 1 : width], arrived(dr, 1)[0:1])
+
+    def inner(r):
+        put(r + 1, cells[r].astype(jnp.float32), cols[0, pl.ds(r, 1), :], cols[1, pl.ds(r, 1), :])
+
+    loop(0, height, inner)
+
+
+def windows(cat, start, rows):
+    width, channels = cat.shape[1:]
+    return jnp.concatenate(
+        [cat[pl.ds(start + a, rows)].reshape(rows * width, channels) for a in range(3)], axis=1
     )
 
 
-def widened(field):
-    return with_halo(field, (("row", 1), ("col", 2)), 1)
-
-
-def kernel_grad(padded, errors):
-    height = errors.shape[1]
-    width = errors.shape[2]
-    rows_out = []
-    for row_off in range(3):
-        cols_out = []
-        for col_off in range(3):
-            window = padded[:, row_off : row_off + height, col_off : col_off + width, :]
-            cols_out.append(
-                jnp.einsum("nhwc,nhwd->cd", window, errors, preferred_element_type=jnp.float32)
-            )
-        rows_out.append(jnp.stack(cols_out))
-    return jnp.stack(rows_out)
+def over_cells(errors, field):
+    return lax.dot_general(errors, field, (((0,), (0,)), ((), ())), preferred_element_type=jnp.float32)
+
+
+def compute_kernel(sizes, block_rows, scenes, cotangent, halo, kernels, out, cat_in, cat_err, cols, flipped, acc_one, acc_two):
+    height, width, channels = scenes.shape
+    taps = 9
+    fill(sizes, 0, scenes, halo, cat_in, cols)
+    fill(sizes, 1, cotangent, halo, cat_err, cols)
+    for t in range(taps):
+        tap = kernels[1, taps - 1 - t].astype(jnp.float32)
+        flipped[t * channels : (t + 1) * channels] = tap.T.astype(flipped.dtype)
+    acc_one[...] = jnp.zeros_like(acc_one)
+    acc_two[...] = jnp.zeros_like(acc_two)
+
+    def step(i):
+        start = i * block_rows
+        fields = windows(cat_in, start, block_rows)
+        errors = windows(cat_err, start, block_rows)
+        pre = jnp.dot(fields, kernels[0].reshape(taps * channels, channels), preferred_element_type=jnp.float32)
+        back = jnp.dot(errors, flipped[...], preferred_element_type=jnp.float32)
+        squash = jax.nn.sigmoid(pre)
+        hidden = (pre * squash).astype(jnp.bfloat16)
+        delta = (back * squash * (1.0 + pre * (1.0 - squash))).astype(jnp.bfloat16)
+        acc_one[...] += over_cells(delta, fields)
+        acc_two[...] += over_cells(hidden, errors)
+
+    loop(0, height // block_rows, step)
+    for t in range(taps):
+        out[t] = acc_one[:, t * channels : (t + 1) * channels].T
+        u = taps - 1 - t
+        out[taps + t] = acc_two[:, u * channels : (u + 1) * channels]
+
+
+def local_grads(sizes, scenes, cotangent, halo, kernels):
+    height, width, channels = scenes.shape
+    block_rows = 8
+    vmem = pl.BlockSpec(memory_space=pltpu.VMEM)
+    cat = pltpu.VMEM((height + 2, width, 3 * channels), jnp.bfloat16)
+    acc = pltpu.VMEM((channels, 9 * channels), jnp.float32)
+    return pl.pallas_call(
+        functools.partial(compute_kernel, sizes, block_rows),
+        out_shape=jax.ShapeDtypeStruct((18, channels, channels), jnp.float32),
+        in_specs=[vmem] * 4,
+        out_specs=vmem,
+        scratch_shapes=[
+            cat,
+            cat,
+            pltpu.VMEM((2, height, channels), jnp.float32),
+            pltpu.VMEM((9 * channels, channels), jnp.bfloat16),
+            acc,
+            acc,
+        ],
+        compiler_params=pltpu.CompilerParams(vmem_limit_bytes=56 * 2**20),
+        name="local_grads",
+    )(scenes, cotangent, halo, kernels)
 
 
 def on_device(sizes, scenes, cotangent, params, partials):
-    whole = perturbed_params(sizes, partials[0], params)
-    channels = scenes.shape[3]
-    kernels = whole.reshape(2, 3, 3, channels, channels)
-    kernel_one = kernels[0]
-    flipped = jnp.transpose(kernels[1][::-1, ::-1], (0, 1, 3, 2))
-    padded_in = widened(scenes)
-    pre = convolve(padded_in, kernel_one)
-    hidden = jax.nn.silu(pre).astype(jnp.bfloat16)
-    back = convolve(widened(cotangent), flipped)
-    squash = jax.nn.sigmoid(pre)
-    delta = (back * squash * (1.0 + pre * (1.0 - squash))).astype(jnp.bfloat16)
-    grad_one = kernel_grad(padded_in, delta)
-    grad_two = kernel_grad(widened(hidden), cotangent)
-    local_grad = jnp.stack([grad_one, grad_two])
-    return scattered_sum(sizes, local_grad)
+    scenes, cotangent = scenes[0], cotangent[0]
+    channels = scenes.shape[2]
+    edges = jnp.stack(
+        [jnp.stack([x[0], x[-1], x[:, 0], x[:, -1]]) for x in (scenes, cotangent)], axis=1
+    )
+    whole, halo = perturbed_params(sizes, partials[0], params, edges)
+    kernels = whole.reshape(2, 9, channels, channels)
+    return scattered_sum(sizes, local_grads(sizes, scenes, cotangent, halo, kernels))
 
 
 def solution(mesh):

time: 177 us -> 71.5 us (0.40)
  other arithmetic: 38.4 us -> 0.69 us
  matrix products: 36.2 us -> 0 us
  starting transfers between devices: 27.3 us -> 0 us
  Pallas kernels: 46.5 us -> 65.3 us
  local copies, waits for them, and re-layouts: 22.6 us -> 4.93 us
  waiting for transfers between devices: 4.66 us -> 0 us
    concatenate x3 -> x0, other arithmetic: 36.9 us -> none  [with_halo(): jnp.concatenate([lax.ppermute(tail, axis, [(i, (i + 1) % count) for i in...]
    ppermute x12 -> x0, starting transfers between devices: 27.3 us -> none  [the longest x6 19.3 us: with_halo(): lax.ppermute(tail, axis, [(i, (i + 1) % count) for i in range(ends)])]
    conv_general_dilated x2 -> x0, matrix products: 27.2 us -> none  [convolve(): lax.conv_general_dilated(padded, kernel, (1, 1), 'VALID', dimension_numbe...]
    pallas_call x1 -> x2, Pallas kernels: 32.2 us -> 50.9 us  [the longest x1 35.8 us: perturbed_params(): pl.pallas_call(functools.partial(perturb_kernel, sizes), out_shape=(jax.S...]
    slice x7 -> x4, local copies, waits for them, and re-layouts: 16 us -> 3.53 us  [the longest x2 2.05 us: on_device(): x[:, 0]]
    dot_general x18 -> x0, matrix products: 8.99 us -> none  [kernel_grad(): jnp.einsum('nhwc,nhwd->cd', window, errors, preferred_element_type=jnp.fl...]
    unnamed x14 -> x3, local copies, waits for them, and re-layouts: 6.41 us -> 1.4 us
    ppermute x12 -> x0, waiting for transfers between devices: 4.66 us -> none  [the longest x6 4.46 us: with_halo(): lax.ppermute(head, axis, [((i + 1) % count, i) for i in range(ends)])]
  transfers between devices with their start and end apart: 12 -> 0, of which waited for: 2 -> 0; matrix products, arithmetic and copies ran while one was open for 16% -> 0% of each run, Pallas kernels for 18% -> 0%
where the time goes in v2:
time: 71.5 us; the launch traced here: 71 us
  Pallas kernels  65.3 us (91%)
  local copies, waits for them, and re-layouts  4.93 us (7%)
    pallas_call x1, Pallas kernels, perturbed_params(): pl.pallas_call(functools.partial(perturb_kernel, sizes), out_shape=(jax.S...  35.8 us
    pallas_call x1, Pallas kernels, local_grads(): pl.pallas_call(functools.partial(compute_kernel, sizes, block_rows), out_...  15.1 us
    pallas_call x1, Pallas kernels, scattered_sum(): pl.pallas_call(functools.partial(scatter_kernel, sizes), out_shape=jax.Sh...  14.4 us
    slice x2, local copies, waits for them, and re-layouts, on_device(): x[:, 0]  2.05 us
    slice x2, local copies, waits for them, and re-layouts, on_device(): x[0]  1.47 us

profile of v2, /device:TPU:0, one launch (start us, length us, event | category | flops | bytes accessed | tf_op | source)
XLA Modules:
  0.0 71.0 jit_solution(8172749122552751552)
XLA Ops:
  0.0 0.7 %slice_bitcast_fusion.3 = (bf16[1,64,128]{2,1,0:T(8,128)(2,1)S(1)}, bf16[1,64,128]{2,1,0:T(8,128)(2,1)S(1)}) fusion(bf16[1,64,64,128]{3,2,1,0:T(8,128)(2,1)} %param.4), kind=kLoop, calls=%fused_computation.10 | loop fusion | bytes 65536 | tf_op jit(solution)/shard_map/slice | solution.py:385
  0.7 0.7 %slice_bitcast_fusion.1 = (bf16[1,64,128]{2,1,0:T(8,128)(2,1)S(1)}, bf16[1,64,128]{2,1,0:T(8,128)(2,1)S(1)}) fusion(bf16[1,64,64,128]{3,2,1,0:T(8,128)(2,1)} %param.5), kind=kLoop, calls=%fused_computation.8 | loop fusion | bytes 65536 | tf_op jit(solution)/shard_map/slice | solution.py:385
  1.5 1.0 %fusion = (bf16[64,1,128]{2,1,0:T(2,128)(2,1)S(1)}, bf16[64,1,128]{2,1,0:T(2,128)(2,1)S(1)}) fusion(bf16[64,64,128]{2,1,0:T(8,128)(2,1)} %bitcast.28), kind=kLoop, calls=%fused_computation.11 | loop fusion | bytes 65536 | tf_op jit(solution)/shard_map/slice | solution.py:385
  2.5 1.0 %fusion.1 = (bf16[64,1,128]{2,1,0:T(2,128)(2,1)S(1)}, bf16[64,1,128]{2,1,0:T(2,128)(2,1)S(1)}) fusion(bf16[64,64,128]{2,1,0:T(8,128)(2,1)} %bitcast.30), kind=kLoop, calls=%fused_computation.12 | loop fusion | bytes 65536 | tf_op jit(solution)/shard_map/slice | solution.py:385
  3.6 0.7 pad_maximum_fusion.edges
  4.3 35.8 %perturb.1 = (bf16[16,2,72,128]{3,2,1,0:T(8,128)(2,1)}, bf16[8,2,64,128]{3,2,1,0:T(8,128)(2,1)}) custom-call(f32[16,2,72,128]{3,2,1,0:T(8,128)} %bitcast.32, f32[72,128]{1,0:T(8,128)} %bitcast.35, bf16[4,2,64,128]{3,2,1,0:T(8,128)(2,1)} %pad_maximum_fusion.edges), custom_call_target="tpu_custom_call" | custom-call | flops 1000000 | bytes 60000000 | tf_op jit(solution)/shard_map/perturb/pallas_call | solution.py:248
  40.1 15.1 %local_grads.1 = f32[18,128,128]{2,1,0:T(8,128)} custom-call(bf16[64,64,128]{2,1,0:T(8,128)(2,1)} %bitcast.29, bf16[64,64,128]{2,1,0:T(8,128)(2,1)} %bitcast.31, bf16[8,2,64,128]{3,2,1,0:T(8,128)(2,1)} %get-tuple-element.7.halo, bf16[2,9,128,128]{3,2,1,0:T(8,128)(2,1)} %bitcast.33), custom_call_target="tpu_custom_call" | custom-call | tf_op jit(solution)/shard_map/local_grads/pallas_call | solution.py:363
  55.2 14.4 %scatter_sum.1 = f32[72,128]{1,0:T(8,128)} custom-call(f32[16,2,72,128]{3,2,1,0:T(8,128)} %bitcast.27), custom_call_target="tpu_custom_call" | custom-call | tf_op jit(solution)/shard_map/scatter_sum/pallas_call | solution.py:274
  69.6 1.4 %copy.24 = f32[9216]{0:T(1024)} copy(f32[9216]{0:T(1024)} %bitcast.34) | data formatting | bytes 73728
  (4 shorter events, 0.0 us)

commit v3 on v2

v3 whole, which is shorter than its diff:
```python
import functools

import jax
import jax.numpy as jnp
from jax import lax
from jax.experimental import pallas as pl
from jax.experimental.pallas import tpu as pltpu
from jax.sharding import PartitionSpec as P

radius = 2.0
epsilon = 1e-06
AXES = ("scene", "row", "col")
MESH = pl.DeviceIdType.MESH
LANES = 128


class Place:
    def __init__(self, sizes):
        self.scenes, self.rows, self.cols = sizes
        self.pairs = self.cols // 2
        self.n = self.scenes * self.rows * self.pairs
        col = lax.axis_index("col")
        self.half = lax.rem(col, 2)
        self.me = (lax.axis_index("scene") * self.rows + lax.axis_index("row")) * self.pairs + col // 2

    def device(self, chip, half):
        return {
            "scene": chip // (self.rows * self.pairs),
            "row": lax.rem(chip // self.pairs, self.rows),
            "col": lax.rem(chip, self.pairs) * 2 + half,
        }

    def after(self, step):
        return lax.rem(self.me + step, self.n)

    def before(self, step):
        return lax.rem(self.me + self.n - step, self.n)


def loop(low, high, body):
    def wrapped(j, carry):
        body(j)
        return carry

    lax.fori_loop(low, high, wrapped, 0)


def wait_all(ref, sem):
    pltpu.make_async_copy(ref, ref, sem).wait()


def greet_all(place):
    barrier = pltpu.get_barrier_semaphore()

    def greet(j):
        chip = place.after(j)
        pl.semaphore_signal(barrier, inc=1, device_id=place.device(chip, place.half), device_id_type=MESH)
        pl.semaphore_signal(barrier, inc=1, device_id=place.device(chip, 1 - place.half), device_id_type=MESH)

    pl.semaphore_signal(barrier, inc=1, device_id=place.device(place.me, 1 - place.half), device_id_type=MESH)
    loop(1, place.n, greet)
    return barrier


def scatter_sum(place, data, own, theirs, sums, landed, swap_send, swap_recv, peer_send, peer_recv):
    n, me, half = place.n, place.me, place.half

    def swap(j):
        chip = place.after(j + 1)
        return pltpu.make_async_remote_copy(
            src_ref=data.at[chip, 1 - half],
            dst_ref=theirs.at[chip],
            send_sem=swap_send,
            recv_sem=swap_recv.at[j],
            device_id=place.device(me, 1 - half),
            device_id_type=MESH,
        )

    loop(0, n, lambda j: swap(j).start())

    def both(j):
        chip = place.after(j + 1)
        mine = own(j, chip)
        swap(j).wait_recv()
        return mine + theirs[chip]

    def pass_on(j):
        sums[j] = both(j).astype(sums.dtype)
        pltpu.make_async_remote_copy(
            src_ref=sums.at[j],
            dst_ref=landed.at[j],
            send_sem=peer_send,
            recv_sem=peer_recv,
            device_id=place.device(place.after(j + 1), half),
            device_id_type=MESH,
        ).start()

    loop(0, n - 1, pass_on)
    total = both(n - 1)
    wait_all(landed, peer_recv)
    total = lax.fori_loop(0, n - 1, lambda j, t: t + landed[j].astype(jnp.float32), total)
    wait_all(theirs, swap_send)
    wait_all(sums, peer_send)
    return total


AROUND = tuple((dr, dc) for dr in (-1, 0, 1) for dc in (-1, 0, 1) if dr or dc)


def edge_of(dr, dc):
    if dr:
        return 1 if dr < 0 else 0
    return 3 if dc < 0 else 2


def start_halo(sizes, edges, halo, halo_send, halo_recv):
    row, col = lax.axis_index("row"), lax.axis_index("col")
    for slot, (dr, dc) in enumerate(AROUND):
        pltpu.make_async_remote_copy(
            src_ref=edges.at[edge_of(dr, dc)],
            dst_ref=halo.at[slot],
            send_sem=halo_send,
            recv_sem=halo_recv,
            device_id={
                "scene": lax.axis_index("scene"),
                "row": lax.rem(row + sizes[1] - dr, sizes[1]),
                "col": lax.rem(col + sizes[2] - dc, sizes[2]),
            },
            device_id_type=MESH,
        ).start()


def fill(sizes, which, cells, halo, cat, cols):
    height, width, channels = cells.shape
    row, col = lax.axis_index("row"), lax.axis_index("col")
    inside_row = {-1: row > 0, 0: row >= 0, 1: row < sizes[1] - 1}
    inside_col = {-1: col > 0, 0: col >= 0, 1: col < sizes[2] - 1}

    def arrived(dr, dc):
        inside = jnp.logical_and(inside_row[dr], inside_col[dc])
        block = halo[AROUND.index((dr, dc)), which].astype(jnp.float32)
        return jnp.where(inside, block, 0.0)

    position = lax.broadcasted_iota(jnp.int32, (width, channels), 0)

    def put(r, line, left, right):
        before = jnp.where(position == 0, left, pltpu.roll(line, 1, 0))
        behind = jnp.where(position == width - 1, right, pltpu.roll(line, width - 1, 0))
        cat[r, :, 0:channels] = before.astype(cat.dtype)
        cat[r, :, channels : 2 * channels] = line.astype(cat.dtype)
        cat[r, :, 2 * channels : 3 * channels] = behind.astype(cat.dtype)

    cols[0] = arrived(0, -1)
    cols[1] = arrived(0, 1)
    for dr, r in ((-1, 0), (1, height + 1)):
        put(r, arrived(dr, 0), arrived(dr, -1)[width - 1 : width], arrived(dr, 1)[0:1])

    def inner(r):
        put(r + 1, cells[r].astype(jnp.float32), cols[0, pl.ds(r, 1), :], cols[1, pl.ds(r, 1), :])

    loop(0, height, inner)


def windows(cat, start, rows):
    width, channels = cat.shape[1:]
    return jnp.concatenate(
        [cat[pl.ds(start + a, rows)].reshape(rows * width, channels) for a in range(3)], axis=1
    )


def over_cells(errors, field):
    return lax.dot_general(errors, field, (((0,), (0,)), ((), ())), preferred_element_type=jnp.float32)


def kernel(sizes, block_rows, data, params, scenes_hbm, cotangent_hbm, out,
           scenes, cotangent, edges, halo, cat_in, cat_err, cols, flat, ones, flipped, acc_one, acc_two, whole, local,
           own, theirs, sums, landed, square, squares, mine, theirs_b, sums_b, landed_b,
           load_sem, own_sem, swap_send, swap_recv, peer_send, peer_recv,
           sq_send, sq_recv, gather_send, gather_recv, relay_send, relay_recv, halo_send, halo_recv,
           swap_send_b, swap_recv_b, peer_send_b, peer_recv_b):
    place = Place(sizes)
    n, me, half = place.n, place.me, place.half
    height, width, channels = scenes.shape
    rows = params.shape[0]
    taps = 9

    loads = [
        pltpu.make_async_copy(scenes_hbm, scenes, load_sem.at[0]),
        pltpu.make_async_copy(cotangent_hbm, cotangent, load_sem.at[1]),
    ]
    for load in loads:
        load.start()

    def load_own(j):
        chip = place.after(j + 1)
        return pltpu.make_async_copy(data.at[chip, half], own.at[chip], own_sem.at[j])

    loop(0, n, lambda j: load_own(j).start())
    barrier = greet_all(place)
    for which, (load, cells) in enumerate(zip(loads, (scenes, cotangent))):
        load.wait()
        edges[0, which] = cells[0]
        edges[1, which] = cells[height - 1]
        edges[2, which] = cells[:, 0:16, :].astype(jnp.float32)[:, 0, :].astype(edges.dtype)
        edges[3, which] = cells[:, width - 16 : width, :].astype(jnp.float32)[:, 15, :].astype(edges.dtype)
    pl.semaphore_wait(barrier, 2 * n - 1)

    def loaded(j, chip):
        load_own(j).wait()
        return own[chip]

    start_halo(sizes, edges, halo, halo_send, halo_recv)
    grads = scatter_sum(place, data, loaded, theirs, sums, landed, swap_send, swap_recv, peer_send, peer_recv)

    square[...] = jnp.full(square.shape, jnp.sum(grads * grads), jnp.float32)

    def tell(chip, to_half, slot):
        pltpu.make_async_remote_copy(
            src_ref=square.at[0],
            dst_ref=squares.at[slot],
            send_sem=sq_send,
            recv_sem=sq_recv,
            device_id=place.device(chip, to_half),
            device_id_type=MESH,
        ).start()

    def tell_chip(j):
        chip = place.after(j)
        tell(chip, half, 2 * j - 1)
        tell(chip, 1 - half, 2 * j)

    loop(1, n, tell_chip)
    tell(me, 1 - half, 0)

    wait_all(halo, halo_recv)
    fill(sizes, 0, scenes, halo, cat_in, cols)
    fill(sizes, 1, cotangent, halo, cat_err, cols)

    wait_all(squares, sq_recv)
    norm2 = square[0] + jnp.sum(squares[...], axis=0)
    factor = radius / (jnp.sqrt(norm2) + epsilon)
    mine[...] = (params[...] + factor * grads).astype(mine.dtype)
    whole[me, half] = mine[...]

    def relay(src, chip):
        return pltpu.make_async_remote_copy(
            src_ref=src,
            dst_ref=whole.at[chip, half],
            send_sem=relay_send,
            recv_sem=relay_recv,
            device_id=place.device(me, 1 - half),
            device_id_type=MESH,
        )

    def give(j):
        return pltpu.make_async_remote_copy(
            src_ref=mine,
            dst_ref=whole.at[me, half],
            send_sem=gather_send,
            recv_sem=gather_recv.at[j],
            device_id=place.device(place.after(j + 1), half),
            device_id_type=MESH,
        )

    loop(0, n - 1, lambda j: give(j).start())
    relay(mine, me).start()

    def hand_over(j):
        chip = place.before(j + 1)
        give(j).wait_recv()
        relay(whole.at[chip, half], chip).start()

    loop(0, n - 1, hand_over)
    wait_all(whole.at[:, 0], relay_recv)
    wait_all(whole.at[:, 0], relay_send)
    wait_all(landed, gather_send)
    wait_all(squares, sq_send)
    wait_all(halo, halo_send)

    def spread(c):
        flat[pl.ds(c * rows, rows), :] = whole[c // 2, lax.rem(c, 2)].astype(jnp.float32)

    loop(0, 2 * n, spread)
    ones[...] = flat[0 : taps * channels].astype(ones.dtype)
    for t in range(taps):
        first = (2 * taps - 1 - t) * channels
        flipped[t * channels : (t + 1) * channels] = flat[first : first + channels].T.astype(flipped.dtype)
    acc_one[...] = jnp.zeros_like(acc_one)
    acc_two[...] = jnp.zeros_like(acc_two)

    def step(i):
        start = i * block_rows
        fields = windows(cat_in, start, block_rows)
        errors = windows(cat_err, start, block_rows)
        pre = jnp.dot(fields, ones[...], preferred_element_type=jnp.float32)
        back = jnp.dot(errors, flipped[...], preferred_element_type=jnp.float32)
        squash = jax.nn.sigmoid(pre)
        hidden = (pre * squash).astype(jnp.bfloat16)
        delta = (back * squash * (1.0 + pre * (1.0 - squash))).astype(jnp.bfloat16)
        acc_one[...] += over_cells(delta, fields)
        acc_two[...] += over_cells(hidden, errors)

    loop(0, height // block_rows, step)
    for t in range(taps):
        flat[t * channels : (t + 1) * channels] = acc_one[:, t * channels : (t + 1) * channels].T
        u = taps - 1 - t
        flat[(taps + t) * channels : (taps + t + 1) * channels] = acc_two[:, u * channels : (u + 1) * channels]

    def collect(c):
        local[c // 2, lax.rem(c, 2)] = flat[pl.ds(c * rows, rows), :]

    loop(0, 2 * n, collect)
    out[...] = scatter_sum(
        place, local, lambda j, chip: local[chip, half], theirs_b, sums_b, landed_b,
        swap_send_b, swap_recv_b, peer_send_b, peer_recv_b,
    )


def on_device(sizes, scenes, cotangent, params, partials):
    scenes, cotangent = scenes[0], cotangent[0]
    height, width, channels = scenes.shape
    n = sizes[0] * sizes[1] * sizes[2] // 2
    rows = params.size // LANES
    dma = pltpu.SemaphoreType.DMA
    half_type, full = jnp.bfloat16, jnp.float32
    anywhere, vmem = pl.BlockSpec(memory_space=pl.ANY), pl.BlockSpec(memory_space=pltpu.VMEM)
    cat = pltpu.VMEM((height + 2, width, 3 * channels), half_type)
    tall = pltpu.VMEM((9 * channels, channels), half_type)
    acc = pltpu.VMEM((channels, 9 * channels), full)
    chunks = [
        pltpu.VMEM((n, rows, LANES), full),
        pltpu.VMEM((n - 1, rows, LANES), half_type),
        pltpu.VMEM((n - 1, rows, LANES), half_type),
    ]
    scratch = [
        pltpu.VMEM(scenes.shape, half_type),
        pltpu.VMEM(scenes.shape, half_type),
        pltpu.VMEM((4, 2, width, channels), half_type),
        pltpu.VMEM((len(AROUND), 2, width, channels), half_type),
        cat,
        cat,
        pltpu.VMEM((2, height, channels), full),
        pltpu.VMEM((18 * channels, channels), full),
        tall,
        tall,
        acc,
        acc,
        pltpu.VMEM((n, 2, rows, LANES), half_type),
        pltpu.VMEM((n, 2, rows, LANES), full),
        pltpu.VMEM((n, rows, LANES), full),
        *chunks,
        pltpu.VMEM((1, 1, LANES), full),
        pltpu.VMEM((2 * n - 1, 1, LANES), full),
        pltpu.VMEM((rows, LANES), half_type),
        *chunks,
        dma((2,)), dma((n,)), dma, dma((n,)), dma, dma,
        dma, dma, dma, dma((n,)), dma, dma, dma, dma,
        dma, dma((n,)), dma, dma,
    ]
    grads = pl.pallas_call(
        functools.partial(kernel, sizes, 8),
        out_shape=jax.ShapeDtypeStruct((rows, LANES), full),
        in_specs=[anywhere, vmem, anywhere, anywhere],
        out_specs=vmem,
        scratch_shapes=scratch,
        compiler_params=pltpu.CompilerParams(
            collective_id=0, has_side_effects=True, vmem_limit_bytes=56 * 2**20
        ),
        name="sam_grad",
    )(partials[0].reshape(n, 2, rows, LANES), params.reshape(rows, LANES), scenes, cotangent)
    return grads.reshape(-1)


def solution(mesh):
    sizes = tuple(mesh.shape[axis] for axis in AXES)
    return jax.shard_map(
        functools.partial(on_device, sizes),
        mesh=mesh,
        in_specs=(
            P("scene", "row", "col", None),
            P("scene", "row", "col", None),
            P(AXES),
            P(AXES, None),
        ),
        out_specs=P(AXES),
        check_vma=False,
    )
```

time: 71.5 us -> 59.1 us (0.83)
  Pallas kernels: 65.3 us -> 57.4 us
  local copies, waits for them, and re-layouts: 4.93 us -> 1.39 us
    pallas_call x3 -> x1, Pallas kernels: 65.3 us -> 57.4 us  [on_device(): pl.pallas_call(functools.partial(kernel, sizes, 8), out_shape=jax.ShapeDt...]
    slice x4 -> x0, local copies, waits for them, and re-layouts: 3.53 us -> none  [the longest x2 2.05 us: on_device(): x[:, 0]]
where the time goes in v3:
time: 59.1 us; the launch traced here: 58.8 us
  Pallas kernels  57.4 us (97%)
  local copies, waits for them, and re-layouts  1.39 us (2%)
    pallas_call x1, Pallas kernels, on_device(): pl.pallas_call(functools.partial(kernel, sizes, 8), out_shape=jax.ShapeDt...  57.4 us
    unnamed x1, local copies, waits for them, and re-layouts  1.39 us

profile of v3, /device:TPU:0, one launch (start us, length us, event | category | flops | bytes accessed | tf_op | source)
XLA Modules:
  0.0 58.8 jit_solution(4626151086679512813)
XLA Ops:
  0.0 57.4 %sam_grad.1 = f32[72,128]{1,0:T(8,128)} custom-call(f32[16,2,72,128]{3,2,1,0:T(8,128)} %bitcast.5, f32[72,128]{1,0:T(8,128)} %bitcast.9, bf16[64,64,128]{2,1,0:T(8,128)(2,1)} %bitcast.6, bf16[64,64,128]{2,1,0:T(8,128)(2,1)} %bitcast.7), custom_call_target="tpu_custom_call" | custom-call | tf_op jit(solution)/shard_map/sam_grad/pallas_call | solution.py:360
  57.5 1.4 %copy.6 = f32[9216]{0:T(1024)} copy(f32[9216]{0:T(1024)} %bitcast.8) | data formatting | bytes 73728

commit v4 on v3

--- a/solution.py
+++ b/solution.py
@@ -21,7 +21,22 @@
         self.n = self.scenes * self.rows * self.pairs
         col = lax.axis_index("col")
         self.half = lax.rem(col, 2)
-        self.me = (lax.axis_index("scene") * self.rows + lax.axis_index("row")) * self.pairs + col // 2
+        self.m = self.scenes * self.pairs
+        self.row = lax.axis_index("row")
+        self.plane = lax.axis_index("scene") * self.pairs + col // 2
+        self.me = self.chip(self.plane, self.row)
+
+    def chip(self, plane, row):
+        return (plane // self.pairs * self.rows + row) * self.pairs + lax.rem(plane, self.pairs)
+
+    def plane_after(self, u):
+        return lax.rem(self.plane + 1 + u, self.m)
+
+    def row_after(self, t):
+        return lax.rem(self.row + 1 + t, self.rows)
+
+    def order(self, j):
+        return self.chip(self.plane_after(lax.rem(j, self.m)), self.row_after(j // self.m))
 
     def device(self, chip, half):
         return {
@@ -33,9 +48,6 @@
     def after(self, step):
         return lax.rem(self.me + step, self.n)
 
-    def before(self, step):
-        return lax.rem(self.me + self.n - step, self.n)
-
 
 def loop(low, high, body):
     def wrapped(j, carry):
@@ -62,11 +74,13 @@
     return barrier
 
 
-def scatter_sum(place, data, own, theirs, sums, landed, swap_send, swap_recv, peer_send, peer_recv):
-    n, me, half = place.n, place.me, place.half
+def scatter_sum(place, data, own, theirs, sums, landed, kept, reached,
+                swap_send, swap_recv, plane_send, plane_recv, row_send, row_recv):
+    n, m, rows, me, half = place.n, place.m, place.rows, place.me, place.half
+    full = jnp.float32
 
     def swap(j):
-        chip = place.after(j + 1)
+        chip = place.order(j)
         return pltpu.make_async_remote_copy(
             src_ref=data.at[chip, 1 - half],
             dst_ref=theirs.at[chip],
@@ -79,28 +93,51 @@
     loop(0, n, lambda j: swap(j).start())
 
     def both(j):
-        chip = place.after(j + 1)
+        chip = place.order(j)
         mine = own(j, chip)
         swap(j).wait_recv()
         return mine + theirs[chip]
 
-    def pass_on(j):
-        sums[j] = both(j).astype(sums.dtype)
+    def across_plane(t):
+        def pass_on(u):
+            slot = t * (m - 1) + u
+            sums[slot] = both(t * m + u).astype(sums.dtype)
+            pltpu.make_async_remote_copy(
+                src_ref=sums.at[slot],
+                dst_ref=landed.at[t, u],
+                send_sem=plane_send,
+                recv_sem=plane_recv.at[t],
+                device_id=place.device(place.chip(place.plane_after(u), place.row), half),
+                device_id_type=MESH,
+            ).start()
+
+        loop(0, m - 1, pass_on)
+        kept[t] = both(t * m + m - 1)
+
+    loop(0, rows, across_plane)
+
+    def plane_total(t):
+        wait_all(landed.at[t], plane_recv.at[t])
+        return lax.fori_loop(0, m - 1, lambda u, sofar: sofar + landed[t, u].astype(full), kept[t])
+
+    def along_rows(t):
+        kept[t] = plane_total(t)
         pltpu.make_async_remote_copy(
-            src_ref=sums.at[j],
-            dst_ref=landed.at[j],
-            send_sem=peer_send,
-            recv_sem=peer_recv,
-            device_id=place.device(place.after(j + 1), half),
+            src_ref=kept.at[t],
+            dst_ref=reached.at[t],
+            send_sem=row_send,
+            recv_sem=row_recv,
+            device_id=place.device(place.chip(place.plane, place.row_after(t)), half),
             device_id_type=MESH,
         ).start()
 
-    loop(0, n - 1, pass_on)
-    total = both(n - 1)
-    wait_all(landed, peer_recv)
-    total = lax.fori_loop(0, n - 1, lambda j, t: t + landed[j].astype(jnp.float32), total)
+    loop(0, rows - 1, along_rows)
+    total = plane_total(rows - 1)
+    wait_all(reached, row_recv)
+    total = lax.fori_loop(0, rows - 1, lambda t, sofar: sofar + reached[t], total)
     wait_all(theirs, swap_send)
-    wait_all(sums, peer_send)
+    wait_all(sums, plane_send)
+    wait_all(reached, row_send)
     return total
 
 
@@ -174,10 +211,12 @@
 
 def kernel(sizes, block_rows, data, params, scenes_hbm, cotangent_hbm, out,
            scenes, cotangent, edges, halo, cat_in, cat_err, cols, flat, ones, flipped, acc_one, acc_two, whole, local,
-           own, theirs, sums, landed, square, squares, mine, theirs_b, sums_b, landed_b,
-           load_sem, own_sem, swap_send, swap_recv, peer_send, peer_recv,
-           sq_send, sq_recv, gather_send, gather_recv, relay_send, relay_recv, halo_send, halo_recv,
-           swap_send_b, swap_recv_b, peer_send_b, peer_recv_b):
+           own, square, squares, mine,
+           theirs, sums, landed, kept, reached, theirs_b, sums_b, landed_b, kept_b, reached_b,
+           load_sem, own_sem,
+           sq_send, sq_recv, gather_send, row_gather, plane_gather, relay_send, relay_recv, halo_send, halo_recv,
+           swap_send, swap_recv, plane_send, plane_recv, row_send, row_recv,
+           swap_send_b, swap_recv_b, plane_send_b, plane_recv_b, row_send_b, row_recv_b):
     place = Place(sizes)
     n, me, half = place.n, place.me, place.half
     height, width, channels = scenes.shape
@@ -192,7 +231,7 @@
         load.start()
 
     def load_own(j):
-        chip = place.after(j + 1)
+        chip = place.order(j)
         return pltpu.make_async_copy(data.at[chip, half], own.at[chip], own_sem.at[j])
 
     loop(0, n, lambda j: load_own(j).start())
@@ -210,7 +249,10 @@
         return own[chip]
 
     start_halo(sizes, edges, halo, halo_send, halo_recv)
-    grads = scatter_sum(place, data, loaded, theirs, sums, landed, swap_send, swap_recv, peer_send, peer_recv)
+    grads = scatter_sum(
+        place, data, loaded, theirs, sums, landed, kept, reached,
+        swap_send, swap_recv, plane_send, plane_recv, row_send, row_recv,
+    )
 
     square[...] = jnp.full(square.shape, jnp.sum(grads * grads), jnp.float32)
 
@@ -252,28 +294,57 @@
             device_id_type=MESH,
         )
 
-    def give(j):
+    m, lines = place.m, place.rows
+
+    def line_before(t):
+        return lax.rem(place.row + 2 * lines - 1 - t, lines)
+
+    def give_row(t):
         return pltpu.make_async_remote_copy(
             src_ref=mine,
             dst_ref=whole.at[me, half],
             send_sem=gather_send,
-            recv_sem=gather_recv.at[j],
-            device_id=place.device(place.after(j + 1), half),
+            recv_sem=row_gather.at[t],
+            device_id=place.device(place.chip(place.plane, place.row_after(t)), half),
             device_id_type=MESH,
         )
 
-    loop(0, n - 1, lambda j: give(j).start())
+    def give_plane(src, chip, t, u):
+        return pltpu.make_async_remote_copy(
+            src_ref=src,
+            dst_ref=whole.at[chip, half],
+            send_sem=gather_send,
+            recv_sem=plane_gather.at[t * (m - 1) + u],
+            device_id=place.device(place.chip(place.plane_after(u), place.row), half),
+            device_id_type=MESH,
+        )
+
+    loop(0, lines - 1, lambda t: give_row(t).start())
+    loop(0, m - 1, lambda u: give_plane(mine, me, lines - 1, u).start())
     relay(mine, me).start()
 
-    def hand_over(j):
-        chip = place.before(j + 1)
-        give(j).wait_recv()
+    def from_row(t):
+        chip = place.chip(place.plane, line_before(t))
+        give_row(t).wait_recv()
+        loop(0, m - 1, lambda u: give_plane(whole.at[chip, half], chip, t, u).start())
         relay(whole.at[chip, half], chip).start()
 
-    loop(0, n - 1, hand_over)
+    loop(0, lines - 1, from_row)
+
+    def from_plane(i):
+        t = lax.rem(i + lines - 1, lines)
+
+        def arrival(u):
+            chip = place.chip(lax.rem(place.plane + 2 * m - 1 - u, m), line_before(t))
+            give_plane(mine, chip, t, u).wait_recv()
+            relay(whole.at[chip, half], chip).start()
+
+        loop(0, m - 1, arrival)
+
+    loop(0, lines, from_plane)
     wait_all(whole.at[:, 0], relay_recv)
     wait_all(whole.at[:, 0], relay_send)
-    wait_all(landed, gather_send)
+    wait_all(whole.at[pl.ds(0, n - 1), 0], gather_send)
     wait_all(squares, sq_send)
     wait_all(halo, halo_send)
 
@@ -311,8 +382,8 @@
 
     loop(0, 2 * n, collect)
     out[...] = scatter_sum(
-        place, local, lambda j, chip: local[chip, half], theirs_b, sums_b, landed_b,
-        swap_send_b, swap_recv_b, peer_send_b, peer_recv_b,
+        place, local, lambda j, chip: local[chip, half], theirs_b, sums_b, landed_b, kept_b, reached_b,
+        swap_send_b, swap_recv_b, plane_send_b, plane_recv_b, row_send_b, row_recv_b,
     )
 
 
@@ -327,11 +398,15 @@
     cat = pltpu.VMEM((height + 2, width, 3 * channels), half_type)
     tall = pltpu.VMEM((9 * channels, channels), half_type)
     acc = pltpu.VMEM((channels, 9 * channels), full)
+    lines, m = sizes[1], n // sizes[1]
     chunks = [
         pltpu.VMEM((n, rows, LANES), full),
-        pltpu.VMEM((n - 1, rows, LANES), half_type),
-        pltpu.VMEM((n - 1, rows, LANES), half_type),
+        pltpu.VMEM((n - lines, rows, LANES), half_type),
+        pltpu.VMEM((lines, m - 1, rows, LANES), half_type),
+        pltpu.VMEM((lines, rows, LANES), full),
+        pltpu.VMEM((lines - 1, rows, LANES), full),
     ]
+    sum_sems = [dma, dma((n,)), dma, dma((lines,)), dma, dma]
     scratch = [
         pltpu.VMEM(scenes.shape, half_type),
         pltpu.VMEM(scenes.shape, half_type),
@@ -348,14 +423,15 @@
         pltpu.VMEM((n, 2, rows, LANES), half_type),
         pltpu.VMEM((n, 2, rows, LANES), full),
         pltpu.VMEM((n, rows, LANES), full),
-        *chunks,
         pltpu.VMEM((1, 1, LANES), full),
         pltpu.VMEM((2 * n - 1, 1, LANES), full),
         pltpu.VMEM((rows, LANES), half_type),
         *chunks,
-        dma((2,)), dma((n,)), dma, dma((n,)), dma, dma,
-        dma, dma, dma, dma((n,)), dma, dma, dma, dma,
-        dma, dma((n,)), dma, dma,
+        *chunks,
+        dma((2,)), dma((n,)),
+        dma, dma, dma, dma((lines - 1,)), dma((n - lines,)), dma, dma, dma, dma,
+        *sum_sems,
+        *sum_sems,
     ]
     grads = pl.pallas_call(
         functools.partial(kernel, sizes, 8),

time: 59.1 us -> 54.7 us (0.926)
  Pallas kernels: 57.4 us -> 53 us
    pallas_call x1, Pallas kernels: 57.4 us -> 53 us  [on_device(): pl.pallas_call(functools.partial(kernel, sizes, 8), out_shape=jax.ShapeDt...]
where the time goes in v4:
time: 54.7 us; the launch traced here: 54.4 us
  Pallas kernels  53 us (97%)
  local copies, waits for them, and re-layouts  1.39 us (3%)
    pallas_call x1, Pallas kernels, on_device(): pl.pallas_call(functools.partial(kernel, sizes, 8), out_shape=jax.ShapeDt...  53 us
    unnamed x1, local copies, waits for them, and re-layouts  1.39 us

profile of v4, /device:TPU:0, one launch (start us, length us, event | category | flops | bytes accessed | tf_op | source)
XLA Modules:
  0.0 54.4 jit_solution(5505315067584417132)
XLA Ops:
  0.0 53.0 %sam_grad.1 = f32[72,128]{1,0:T(8,128)} custom-call(f32[16,2,72,128]{3,2,1,0:T(8,128)} %bitcast.5, f32[72,128]{1,0:T(8,128)} %bitcast.9, bf16[64,64,128]{2,1,0:T(8,128)(2,1)} %bitcast.6, bf16[64,64,128]{2,1,0:T(8,128)(2,1)} %bitcast.7), custom_call_target="tpu_custom_call" | custom-call | tf_op jit(solution)/shard_map/sam_grad/pallas_call | solution.py:436
  53.1 1.4 %copy.6 = f32[9216]{0:T(1024)} copy(f32[9216]{0:T(1024)} %bitcast.8) | data formatting | bytes 73728

commit v5 on v4

--- a/solution.py
+++ b/solution.py
@@ -49,12 +49,12 @@
         return lax.rem(self.me + step, self.n)
 
 
-def loop(low, high, body):
+def loop(low, high, body, unroll=1):
     def wrapped(j, carry):
         body(j)
         return carry
 
-    lax.fori_loop(low, high, wrapped, 0)
+    lax.fori_loop(low, high, wrapped, 0, unroll=unroll)
 
 
 def wait_all(ref, sem):
@@ -195,7 +195,7 @@
     def inner(r):
         put(r + 1, cells[r].astype(jnp.float32), cols[0, pl.ds(r, 1), :], cols[1, pl.ds(r, 1), :])
 
-    loop(0, height, inner)
+    loop(0, height, inner, unroll=4)
 
 
 def windows(cat, start, rows):
@@ -276,7 +276,6 @@
 
     wait_all(halo, halo_recv)
     fill(sizes, 0, scenes, halo, cat_in, cols)
-    fill(sizes, 1, cotangent, halo, cat_err, cols)
 
     wait_all(squares, sq_recv)
     norm2 = square[0] + jnp.sum(squares[...], axis=0)
@@ -322,6 +321,7 @@
     loop(0, lines - 1, lambda t: give_row(t).start())
     loop(0, m - 1, lambda u: give_plane(mine, me, lines - 1, u).start())
     relay(mine, me).start()
+    fill(sizes, 1, cotangent, halo, cat_err, cols)
 
     def from_row(t):
         chip = place.chip(place.plane, line_before(t))
@@ -351,7 +351,7 @@
     def spread(c):
         flat[pl.ds(c * rows, rows), :] = whole[c // 2, lax.rem(c, 2)].astype(jnp.float32)
 
-    loop(0, 2 * n, spread)
+    loop(0, 2 * n, spread, unroll=4)
     ones[...] = flat[0 : taps * channels].astype(ones.dtype)
     for t in range(taps):
         first = (2 * taps - 1 - t) * channels
@@ -380,7 +380,7 @@
     def collect(c):
         local[c // 2, lax.rem(c, 2)] = flat[pl.ds(c * rows, rows), :]
 
-    loop(0, 2 * n, collect)
+    loop(0, 2 * n, collect, unroll=4)
     out[...] = scatter_sum(
         place, local, lambda j, chip: local[chip, half], theirs_b, sums_b, landed_b, kept_b, reached_b,
         swap_send_b, swap_recv_b, plane_send_b, plane_recv_b, row_send_b, row_recv_b,

time: 54.7 us -> 54.4 us (level)
  no operation moved by 1% of the time
where the time goes in v5:
time: 54.4 us; the launch traced here: 54.1 us
  Pallas kernels  52.8 us (97%)
  local copies, waits for them, and re-layouts  1.39 us (3%)
    pallas_call x1, Pallas kernels, on_device(): pl.pallas_call(functools.partial(kernel, sizes, 8), out_shape=jax.ShapeDt...  52.8 us
    unnamed x1, local copies, waits for them, and re-layouts  1.39 us

profile of v5, /device:TPU:0, one launch (start us, length us, event | category | flops | bytes accessed | tf_op | source)
XLA Modules:
  0.0 54.1 jit_solution(4959130095577730943)
XLA Ops:
  0.0 52.8 %sam_grad.1 = f32[72,128]{1,0:T(8,128)} custom-call(f32[16,2,72,128]{3,2,1,0:T(8,128)} %bitcast.5, f32[72,128]{1,0:T(8,128)} %bitcast.9, bf16[64,64,128]{2,1,0:T(8,128)(2,1)} %bitcast.6, bf16[64,64,128]{2,1,0:T(8,128)(2,1)} %bitcast.7), custom_call_target="tpu_custom_call" | custom-call | tf_op jit(solution)/shard_map/sam_grad/pallas_call | solution.py:436
  52.8 1.4 %copy.6 = f32[9216]{0:T(1024)} copy(f32[9216]{0:T(1024)} %bitcast.8) | data formatting | bytes 73728

commit v6 on v5

--- a/solution.py
+++ b/solution.py
@@ -434,7 +434,7 @@
         *sum_sems,
     ]
     grads = pl.pallas_call(
-        functools.partial(kernel, sizes, 8),
+        functools.partial(kernel, sizes, 16),
         out_shape=jax.ShapeDtypeStruct((rows, LANES), full),
         in_specs=[anywhere, vmem, anywhere, anywhere],
         out_specs=vmem,

time: 54.4 us -> 52.8 us (0.971)
  Pallas kernels: 52.8 us -> 51.1 us
    pallas_call x1, Pallas kernels: 52.8 us -> 51.1 us  [on_device(): pl.pallas_call(functools.partial(kernel, sizes, 16), out_shape=jax.ShapeD...]
where the time goes in v6:
time: 52.8 us; the launch traced here: 52.5 us
  Pallas kernels  51.1 us (97%)
  local copies, waits for them, and re-layouts  1.39 us (3%)
    pallas_call x1, Pallas kernels, on_device(): pl.pallas_call(functools.partial(kernel, sizes, 16), out_shape=jax.ShapeD...  51.1 us
    unnamed x1, local copies, waits for them, and re-layouts  1.39 us

profile of v6, /device:TPU:0, one launch (start us, length us, event | category | flops | bytes accessed | tf_op | source)
XLA Modules:
  0.0 52.5 jit_solution(1370122982757562737)
XLA Ops:
  0.0 51.1 %sam_grad.1 = f32[72,128]{1,0:T(8,128)} custom-call(f32[16,2,72,128]{3,2,1,0:T(8,128)} %bitcast.5, f32[72,128]{1,0:T(8,128)} %bitcast.9, bf16[64,64,128]{2,1,0:T(8,128)(2,1)} %bitcast.6, bf16[64,64,128]{2,1,0:T(8,128)(2,1)} %bitcast.7), custom_call_target="tpu_custom_call" | custom-call | tf_op jit(solution)/shard_map/sam_grad/pallas_call | solution.py:436
  51.1 1.4 %copy.6 = f32[9216]{0:T(1024)} copy(f32[9216]{0:T(1024)} %bitcast.8) | data formatting | bytes 73728
